TPU v7x, 128 devices: a whole 4x4x4 slice. The times are simulated.
128 devices in a mesh: rel: 4 (over z), ent: 32 (over y, x, core).
Axes of the slice: x: 4, y: 4, z: 4, core: 2. Of those that a mesh axis runs over, the one named last changes fastest.
Arguments:
- features: bfloat16 [16384, 512], P('ent'), may hold values from -6 to 6
- w_self: bfloat16 [512, 512], replicated, may hold values from -0.25 to 0.25
- basis_mats: bfloat16 [16384, 512], replicated, may hold values from -0.046875 to 0.046875
- basis_coeffs: float32 [1000, 32], replicated, may hold values from -5 to 5
- group_rels: int32 [1000], P('rel'), may hold values from 0 to 999, each once
- rel_local: int32 [65536], P(('rel', 'ent')), may hold values from 0 to 249
- edge_src: int32 [65536], P(('rel', 'ent')), may hold values from 0 to 16383, as said below
- edge_dst: int32 [65536], P(('rel', 'ent')), may hold values from 0 to 16383, as said below
- block_counts: int32 [4, 32, 32], P('rel', 'ent'), may hold values from 1 to 16, as said below
- cotangent: bfloat16 [16384, 512], P('ent'), may hold values from -6 to 6
Outputs:
- activations: bfloat16 [16384, 512], P('ent')
- grad_features: bfloat16 [16384, 512], P('ent')
- grad_basis: float32 [16384, 512], P(('rel', 'ent'))
Inputs may be any that keep to these rules, and one draw needn't show every extreme that they name: `edge_src`: slot i's source is owned by ent index (i // 512) % 32: it lies in [that index * 512, that index * 512 + 512). `edge_dst`: slot i's destination is owned by block index k = (i % 512) // 16: it lies in [k * 512, k * 512 + 512); within each aligned block of 16 slots the destinations are non-decreasing; the live slots of a block are its first block_counts ones. `block_counts`: one relation group, drawn from the seed, has every block full.
All inputs are finite; a program needn't handle non-finite values.
Results may differ from a plain program's by a relative error of at most 0.0059.
Values may be sent and summed in bfloat16 or wider, within the bound.
A program may use at most 192 MiB of HBM per device.

v0:
```python
import jax
import jax.numpy as jnp
from jax import lax
from jax.sharding import PartitionSpec as P


def activate(features, w_self, partial_sums, in_degree, cotangent):
    inverse = 1.0 / jnp.maximum(in_degree, 1.0)
    pre_act = (
        jnp.dot(features, w_self, preferred_element_type=jnp.float32)
        + partial_sums * inverse[:, None]
    )
    sigmoid_pre = jax.nn.sigmoid(pre_act)
    out_rows = (pre_act * sigmoid_pre).astype(jnp.bfloat16)
    grad_pre = (
        cotangent.astype(jnp.float32) * (sigmoid_pre * (1.0 + pre_act * (1.0 - sigmoid_pre)))
    ).astype(jnp.bfloat16)
    grad_scaled = (grad_pre.astype(jnp.float32) * inverse[:, None]).astype(jnp.bfloat16)
    return (out_rows, grad_pre, grad_scaled)


def per_device(
    features,
    w_self,
    basis_mats,
    basis_coeffs,
    group_rels,
    rel_local,
    edge_src,
    edge_dst,
    block_counts,
    cotangent,
):
    ent_dev, feat_width = features.shape
    ent_count = lax.axis_size("ent")
    slot_count = rel_local.shape[0]
    block_cap = slot_count // ent_count
    basis_count = basis_coeffs.shape[1]
    first_row = lax.axis_index("ent") * ent_dev
    slot_index = jnp.arange(slot_count, dtype=jnp.int32)
    limits = jnp.repeat(block_counts.reshape(ent_count), block_cap, total_repeat_length=slot_count)
    is_live = slot_index % block_cap < limits
    rel_coef = basis_coeffs[group_rels[rel_local]]
    src_local = edge_src - first_row
    src_rows = features[src_local].astype(jnp.float32)
    mixed_rows = (
        (rel_coef[:, :, None] * src_rows[:, None, :])
        .reshape(slot_count, basis_count * feat_width)
        .astype(jnp.bfloat16)
    )
    product = jnp.dot(mixed_rows, basis_mats, preferred_element_type=jnp.float32)
    messages = (product * is_live.astype(jnp.float32)[:, None]).astype(jnp.bfloat16)
    owner_base = slot_index // block_cap * ent_dev
    targets = jnp.where(is_live, edge_dst - owner_base, ent_dev)
    arrived, dest_slots = (
        lax.all_to_all(
            messages.reshape(ent_count, block_cap, feat_width),
            "ent",
            split_axis=0,
            concat_axis=0,
            tiled=True,
        ),
        lax.all_to_all(
            targets.reshape(ent_count, block_cap), "ent", split_axis=0, concat_axis=0, tiled=True
        ),
    )
    arrived = arrived.reshape(slot_count, feat_width)
    dest_slots = dest_slots.reshape(slot_count)
    one_hot = (dest_slots[None, :] == jnp.arange(ent_dev, dtype=jnp.int32)[:, None]).astype(
        jnp.bfloat16
    )
    partial_sums = jnp.dot(one_hot, arrived, preferred_element_type=jnp.float32)
    in_degree = jnp.sum(one_hot, axis=1, dtype=jnp.float32)
    partial_sums, in_degree = lax.psum((partial_sums, in_degree), "rel")
    out_rows, grad_pre, grad_scaled = activate(features, w_self, partial_sums, in_degree, cotangent)
    picked = grad_scaled[jnp.minimum(dest_slots, ent_dev - 1)]
    grad_back = jnp.where((dest_slots < ent_dev)[:, None], picked, jnp.zeros((), jnp.bfloat16))
    returned = lax.all_to_all(
        grad_back.reshape(ent_count, block_cap, feat_width),
        "ent",
        split_axis=0,
        concat_axis=0,
        tiled=True,
    )
    returned = returned.reshape(slot_count, feat_width)
    grad_mixed = lax.dot_general(
        returned, basis_mats, (((1,), (1,)), ((), ())), preferred_element_type=jnp.float32
    )
    grad_rows = jnp.sum(
        grad_mixed.reshape(slot_count, basis_count, feat_width) * rel_coef[:, :, None], axis=1
    )
    grad_src = jax.ops.segment_sum(grad_rows, src_local, ent_dev)
    grad_src = lax.psum(grad_src, "rel")
    self_part = lax.dot_general(
        grad_pre, w_self, (((1,), (1,)), ((), ())), preferred_element_type=jnp.float32
    )
    grad_features = (self_part + grad_src).astype(jnp.bfloat16)
    grad_basis = lax.psum_scatter(
        lax.dot_general(
            mixed_rows, returned, (((0,), (0,)), ((), ())), preferred_element_type=jnp.float32
        ),
        ("rel", "ent"),
        scatter_dimension=0,
        tiled=True,
    )
    return (out_rows, grad_features, grad_basis)


def solution(mesh):
    placed = (
        P("ent", None),
        P(),
        P(),
        P(),
        P("rel"),
        P(("rel", "ent")),
        P(("rel", "ent")),
        P(("rel", "ent")),
        P("rel", "ent", None),
        P("ent", None),
    )
    return jax.shard_map(
        per_device,
        mesh=mesh,
        in_specs=placed,
        out_specs=(P("ent", None), P("ent", None), P(("rel", "ent"), None)),
        check_vma=False,
    )
```

profile of v0, /device:TPU:0, one launch (start us, length us, event | category | flops | bytes accessed | tf_op | source)
XLA Modules:
  0.0 951.0 jit_solution(16518272372429316720)
XLA Ops:
  7.2 0.0 copy-start
  7.2 1.8 fusion.18
  9.0 2.1 fusion.17
  11.1 0.8 add_add_fusion.1
  11.9 4.5 compare_select_fusion.3
  16.4 0.2 compare_reduce_fusion.24
  16.5 16.4 %fusion.11 = (s32[512]{0:T(512)S(1)}, pred[512]{0:T(512)(128)(4,1)S(1)}) fusion(s32[512]{0:T(512)} %param.19, pred[512]{0:T(512)(128)(4,1)S(1)} %get-tuple-element.41, pred[512]{0:T(512)(128)(4,1)S(1)} %get-tuple-element.40, pred[512]{0:T(512)(128)(4,1)S(1)} %get-tuple-element.39, pred[512]{0:T(512)(128)(4,1)S(1)} %get-tuple-element.38, ...), kind=kLoop, calls=%fused_computation.77 | loop fusion | flops 25600 | bytes 21620 | tf_op jit(solution)/shard_map/jit(_where)/select_n | solution.py:54
  32.9 0.7 all_to_all.12
  33.6 7.4 all-to-all-start
  41.0 0.7 compare_select_fusion.10
  41.7 3.6 gather_fusion
  45.3 0.7 compare_select_fusion.9
  46.0 1.1 copy.29
  47.1 1.0 gather_fusion.1
  48.2 0.1 copy.30
  48.3 0.0 copy-done
  48.3 2.0 gather_fusion.2
  50.3 0.1 convert_element_type.54
  50.4 6.1 multiply_convert_fusion
  56.5 22.5 %copy.31 = bf16[512,32,512]{0,2,1:T(8,128)(2,1)} copy(bf16[512,32,512]{2,0,1:T(8,128)(2,1)} %multiply_convert_fusion) | data formatting | bytes 33554432 | tf_op jit(solution)/shard_map/convert_element_type | solution.py:49
  79.0 0.0 copy-start.2
  79.0 0.0 copy-start.3
  79.0 18.1 %fusion.1 = bf16[512,512]{1,0:T(8,128)(2,1)} fusion(bf16[512,16384]{0,1:T(8,128)(2,1)} %bitcast.70, bf16[16384,512]{1,0:T(8,128)(2,1)} %param.14, f32[512]{0:T(512)S(1)} %convert_element_type.57), kind=kOutput, calls=%fused_computation.11 | convolution fusion | flops 8590458880 | bytes 34080768 | tf_op jit(solution)/shard_map/dot_general | solution.py:51
  97.0 0.0 all-to-all-done
  97.0 7.4 all-to-all-start.1
  104.4 0.0 all-reduce.3.cloned.1.call-start
  104.5 0.5 broadcast.478
  105.0 0.7 minimum_reduce_fusion
  105.7 0.1 eq.17
  105.8 10.4 %all-to-all-done.1 = bf16[32,16,512]{2,1,0:T(8,128)(2,1)S(1)} async-done(((bf16[32,16,512]{2,1,0:T(8,128)(2,1)}), bf16[32,16,512]{2,1,0:T(8,128)(2,1)S(1)}, u32[]{:S(2)}, u32[]{:S(2)}) %all-to-all-start.1) | async-done | bytes 524320 | tf_op jit(solution)/shard_map/all_to_all | solution.py:56
  116.2 1.5 fusion.3
  117.7 0.0 all-reduce.3.cloned.1.call-update
  117.7 0.0 all-reduce.5.cloned.1.call-start
  117.7 0.1 copy.32
  117.8 0.1 copy.33
  117.9 0.1 min.18
  118.0 0.2 convert_reduce_fusion
  118.2 12.0 %psum.22 = f32[512]{0:T(512)S(1)} all-reduce(f32[512]{0:T(512)S(1)} %convert_reduce_fusion), channel_id=1, replica_groups=mesh['rel'=4,'ent'=32] {'rel'}, use_global_device_ids=true, to_apply=%region_2.3 | all-reduce | flops 512 | bytes 4096 | tf_op jit(solution)/shard_map/psum | solution.py:74
  130.2 32.6 %all-reduce.3.cloned.1.call-done = f32[512,512]{1,0:T(8,128)} async-done(((f32[512,512]{1,0:T(8,128)}), f32[512,512]{1,0:T(8,128)}) %all-reduce.3.cloned.1.call-update) | async-done | bytes 1048592 | tf_op jit(solution)/shard_map/psum | solution.py:74
  162.8 0.0 copy-done.2
  162.8 0.0 copy-done.3
  162.8 2.9 multiply_convert_fusion.1
  165.6 2.0 gather_fusion.3
  167.6 0.1 broadcast_select_fusion
  167.8 18.7 %all_to_all.19 = bf16[32,16,512]{2,1,0:T(8,128)(2,1)S(1)} all-to-all(bf16[32,16,512]{2,1,0:T(8,128)(2,1)S(1)} %broadcast_select_fusion), channel_id=1, replica_groups=mesh['rel'=4,'ent'=32] {'ent'}, dimensions={0} | all-to-all | bytes 1048576 | tf_op jit(solution)/shard_map/all_to_all | solution.py:78
  186.4 12.7 %multiply_reduce_fusion = f32[512,512]{1,0:T(8,128)S(1)} fusion(f32[512,32]{0,1:T(8,128)S(1)} %copy.30, bf16[512,512,1]{1,0,2:T(8,128)(2,1)S(1)} %bitcast.74, bf16[32,512,512]{2,1,0:T(8,128)(2,1)} %bitcast.82), kind=kOutput, calls=%fused_computation.5 | convolution fusion | flops 8606449664 | bytes 18415616 | tf_op jit(solution)/shard_map/dot_general | solution.py:86
  199.1 4.6 scatter_custom_fusion
  203.7 0.0 all-reduce.5.cloned.1.call-update
  203.7 0.3 reduce-scatter.2.cloned.1.call-start
  204.0 21.5 %fusion.19 = f32[16384,512]{1,0:T(8,128)} fusion(bf16[512,16384]{0,1:T(8,128)(2,1)} %bitcast.71, bf16[512,512]{1,0:T(8,128)(2,1)S(1)} %bitcast.75), kind=kOutput, calls=%fused_computation.89 | convolution fusion | flops 8589934592 | bytes 50855936 | tf_op jit(solution)/shard_map/dot_general | solution.py:99
  225.5 0.0 copy-start.1
  225.5 0.0 reduce-scatter.2.cloned.1.call-update
  225.5 21.8 %all-reduce.5.cloned.1.call-done = f32[512,512]{1,0:T(8,128)} async-done(((f32[512,512]{1,0:T(8,128)}), f32[512,512]{1,0:T(8,128)}) %all-reduce.5.cloned.1.call-update) | async-done | bytes 1048592 | tf_op jit(solution)/shard_map/psum | solution.py:93
  247.3 2.5 fusion
  249.8 694.7 %reduce-scatter.2.cloned.1.call-done = f32[128,512]{1,0:T(8,128)} async-done(((f32[16384,512]{1,0:T(8,128)}), f32[128,512]{1,0:T(8,128)}) %reduce-scatter.2.cloned.1.call-update) | async-done | bytes 262160 | tf_op jit(solution)/shard_map/reduce_scatter | solution.py:98
  944.5 0.0 copy-done.1
  (10 shorter events, 0.1 us)
Async XLA Ops:
  7.2 41.1 %copy-start = (bf16[512,512]{1,0:T(8,128)(2,1)S(1)}, bf16[512,512]{1,0:T(8,128)(2,1)}, u32[]{:S(2)}) copy-start(bf16[512,512]{1,0:T(8,128)(2,1)} %param.12) | copy-start | bytes 1572868
  33.6 63.5 %all-to-all-start = ((s32[32,1,16]{2,1,0:T(1,128)}), s32[32,1,16]{2,1,0:T(1,128)S(1)}, u32[]{:S(2)}, u32[]{:S(2)}) async-start(s32[32,1,16]{2,1,0:T(1,128)} %bitcast.37), calls=%async_computation | async-start | bytes 32768 | tf_op jit(solution)/shard_map/all_to_all | solution.py:63
  79.0 83.8 %copy-start.2 = (bf16[512,512]{1,0:T(8,128)(2,1)S(1)}, bf16[512,512]{1,0:T(8,128)(2,1)}, u32[]{:S(2)}) copy-start(bf16[512,512]{1,0:T(8,128)(2,1)} %param.13) | copy-start | bytes 1572868
  79.0 83.8 %copy-start.3 = (bf16[512,512]{1,0:T(8,128)(2,1)S(1)}, bf16[512,512]{1,0:T(8,128)(2,1)}, u32[]{:S(2)}) copy-start(bf16[512,512]{1,0:T(8,128)(2,1)} %param.21) | copy-start | bytes 1572868
  97.0 19.1 %all-to-all-start.1 = ((bf16[32,16,512]{2,1,0:T(8,128)(2,1)}), bf16[32,16,512]{2,1,0:T(8,128)(2,1)S(1)}, u32[]{:S(2)}, u32[]{:S(2)}) async-start(bf16[32,16,512]{2,1,0:T(8,128)(2,1)} %bitcast.41), calls=%async_computation.1 | async-start | bytes 1048576 | tf_op jit(solution)/shard_map/all_to_all | solution.py:56
  104.4 58.3 %all-reduce.3.cloned.1.call-start = ((), (), s32[]{:S(2)}) async-start(), calls=%async_computation.4 | async-start | bytes 2097152 | tf_op jit(solution)/shard_map/psum | solution.py:74
  117.7 129.6 %all-reduce.5.cloned.1.call-start = ((), (), s32[]{:S(2)}) async-start(), calls=%async_computation.5 | async-start | bytes 2097152 | tf_op jit(solution)/shard_map/psum | solution.py:93
  203.7 740.8 %reduce-scatter.2.cloned.1.call-start = ((), (), s32[]{:S(2)}) async-start(), calls=%async_computation.6 | async-start | bytes 33816576 | tf_op jit(solution)/shard_map/reduce_scatter | solution.py:98
  225.5 719.0 %copy-start.1 = (bf16[512,512]{1,0:T(8,128)(2,1)S(1)}, bf16[512,512]{1,0:T(8,128)(2,1)}, u32[]{:S(2)}) copy-start(bf16[512,512]{1,0:T(8,128)(2,1)} %param.12) | copy-start | bytes 1572868
Sparse Core Ops, SparseCore 0:
  117.8 44.9 all-reduce.2
  203.8 43.4 all-reduce.4
  250.3 694.1 reduce-scatter.1
where the time goes:
time: 952 us; the launch traced here: 951 us
  waiting for transfers between devices  759 us (80%)
  matrix products  59.1 us (6%)
  local copies, waits for them, and re-layouts  37.8 us (4%)
  other arithmetic  35 us (4%)
  blocking collectives  30.7 us (3%)
  starting transfers between devices  15.1 us (2%)
  between operations  13.9 us (1%)
    reduce_scatter x1, waiting for transfers between devices, per_device(): lax.psum_scatter(lax.dot_general(mixed_rows, returned, (((0,), (0,)), (()...  695 us
    psum x1, waiting for transfers between devices, per_device(): partial_sums, in_degree = lax.psum((partial_sums, in_degree), 'rel')  32.6 us
    convert_element_type x1, local copies, waits for them, and re-layouts, per_device(): mixed_rows = (rel_coef[:, :, None] * src_rows[:, None, :]).reshape(slot_c...  22.5 us
    psum x1, waiting for transfers between devices, per_device(): grad_src = lax.psum(grad_src, 'rel')  21.8 us
    dot_general x1, matrix products, per_device(): lax.dot_general(mixed_rows, returned, (((0,), (0,)), ((), ())), preferred...  21.5 us
  transfers between devices with their start and end apart: 5, of which 4 were waited for; matrix products, arithmetic and copies ran while one was open for 9% of the time, Pallas kernels for 0%

commit v1 on v0

v1 whole, which is shorter than its diff:
```python
import jax
import jax.numpy as jnp
from jax import lax
from jax.sharding import PartitionSpec as P

BF = jnp.bfloat16
F32 = jnp.float32


def dot(a, b, dims=((1,), (0,)), precision=None):
    return lax.dot_general(
        a, b, (dims, ((), ())), preferred_element_type=F32, precision=precision
    )


def swap(x, axis):
    return lax.all_to_all(x, axis, split_axis=0, concat_axis=0, tiled=True)


def per_device(
    features,
    w_self,
    basis_mats,
    basis_coeffs,
    group_rels,
    rel_local,
    edge_src,
    edge_dst,
    block_counts,
    cotangent,
):
    n_ent, width = features.shape
    ent_count = lax.axis_size("ent")
    rel_count = lax.axis_size("rel")
    slots = rel_local.shape[0]
    cap = slots // ent_count
    bases = basis_coeffs.shape[1]
    rels = basis_coeffs.shape[0]
    part = width // rel_count
    q = lax.axis_index("rel")
    s = lax.axis_index("ent")
    all_slots = slots * rel_count

    pos = jnp.arange(slots, dtype=jnp.int32)
    limits = jnp.repeat(block_counts.reshape(ent_count), cap, total_repeat_length=slots)
    live = pos % cap < limits
    src_own = edge_src - s * n_ent
    dst_own = jnp.where(live, edge_dst - pos // cap * n_ent, n_ent)
    rel_own = group_rels[rel_local]
    meta = jnp.stack([src_own, dst_own, rel_own])
    meta = lax.all_gather(meta, "rel").reshape(rel_count, 3, ent_count, cap)
    meta = meta.transpose(2, 1, 0, 3)
    src = meta[:, 0].reshape(all_slots)
    arrived = swap(meta[:, 1:], "ent")
    dst = arrived[:, 0].reshape(all_slots)
    rel = arrived[:, 1].reshape(all_slots)

    ids = jnp.arange(n_ent, dtype=jnp.int32)[:, None]
    pick_src = (ids == src[None, :]).astype(BF)
    feat_part = lax.dynamic_slice_in_dim(features, q * part, part, 1)
    rows = dot(pick_src, feat_part, ((0,), (0,))).astype(BF)
    rows = swap(rows.reshape(ent_count, rel_count * cap, part), "ent").reshape(all_slots, part)

    pick_rel = (jnp.arange(rels, dtype=jnp.int32)[:, None] == rel[None, :]).astype(F32)
    coef_t = dot(basis_coeffs, pick_rel, ((0,), (0,)), lax.Precision.HIGHEST)
    pick = (ids == dst[None, :]).astype(BF)
    degree = jnp.sum(pick, axis=1, dtype=F32)
    inverse = (1.0 / jnp.maximum(degree, 1.0))[:, None]
    mixed_t = (
        (coef_t[:, None, :] * rows.T.astype(F32)[None])
        .reshape(bases * part, all_slots)
        .astype(BF)
    )
    agg = dot(pick, mixed_t, ((1,), (1,))).astype(BF)
    basis_part = lax.dynamic_slice_in_dim(
        basis_mats.reshape(bases, width, width), q * part, part, 1
    ).reshape(bases * part, width)
    partial = dot(agg, basis_part).astype(BF)
    partial = swap(partial.reshape(n_ent, rel_count, part).transpose(1, 0, 2), "rel")
    sums = jnp.sum(partial.astype(F32), axis=0)

    w_part = lax.dynamic_slice_in_dim(w_self, q * part, part, 1)
    cot = lax.dynamic_slice_in_dim(cotangent, q * part, part, 1).astype(F32)
    pre = dot(features, w_part) + sums * inverse
    sig = jax.nn.sigmoid(pre)
    act = (pre * sig).astype(BF)
    grad_pre = (cot * (sig * (1.0 + pre * (1.0 - sig)))).astype(BF)
    act = lax.all_gather(act, "rel", axis=1, tiled=True)
    grad_pre = lax.all_gather(grad_pre, "rel", axis=1, tiled=True)
    scaled = (grad_pre.astype(F32) * inverse).astype(BF)

    basis_terms = dot(agg, scaled, ((0,), (0,))).astype(BF)
    basis_terms = swap(basis_terms.reshape(ent_count, part, width), "ent")
    block = jnp.sum(basis_terms.astype(F32), axis=0)
    per_rel = bases // rel_count
    routes = [
        (r * ent_count + b, (b // per_rel) * ent_count + (b % per_rel) * rel_count + r)
        for r in range(rel_count)
        for b in range(bases)
    ]
    grad_basis = lax.ppermute(block, ("rel", "ent"), routes)

    back_t = dot(basis_part, scaled, ((1,), (1,))).astype(BF)
    spread = dot(back_t, pick).reshape(bases, part, all_slots)
    grad_rows = jnp.sum(spread * coef_t[:, None, :], axis=0).astype(BF).T
    grad_rows = swap(grad_rows.reshape(ent_count, rel_count * cap, part), "ent")
    w_rows = lax.dynamic_slice_in_dim(w_self, q * part, part, 0)
    grad_part = dot(grad_pre, w_rows, ((1,), (1,))) + dot(
        pick_src, grad_rows.reshape(all_slots, part)
    )
    grad_features = lax.all_gather(grad_part.astype(BF), "rel", axis=1, tiled=True)
    return act, grad_features, grad_basis


def solution(mesh):
    placed = (
        P("ent", None),
        P(),
        P(),
        P(),
        P("rel"),
        P(("rel", "ent")),
        P(("rel", "ent")),
        P(("rel", "ent")),
        P("rel", "ent", None),
        P("ent", None),
    )
    return jax.shard_map(
        per_device,
        mesh=mesh,
        in_specs=placed,
        out_specs=(P("ent", None), P("ent", None), P(("rel", "ent"), None)),
        check_vma=False,
    )
```

time: 952 us -> 230 us (0.24)
  the two profiles are of different devices: /device:TPU:0 before, /device:TPU:25 now
where the time goes in v1:
time: 230 us; the launch traced here: 228 us
  matrix products  51.8 us (23%)
  blocking collectives  48.4 us (21%)
  other arithmetic  46.6 us (20%)
  starting transfers between devices  45.6 us (20%)
  local copies, waits for them, and re-layouts  19 us (8%)
  waiting for transfers between devices  15.6 us (7%)
    dot_general x10, matrix products, dot(): lax.dot_general(a, b, (dims, ((), ())), preferred_element_type=F32, preci...  51.8 us
    all_to_all x5, starting transfers between devices, swap(): return lax.all_to_all(x, axis, split_axis=0, concat_axis=0, tiled=True)  40.3 us
    select_n x1, other arithmetic, per_device(): dst_own = jnp.where(live, edge_dst - pos // cap * n_ent, n_ent)  16.4 us
    all_gather x1, blocking collectives, per_device(): lax.all_gather(grad_part.astype(BF), 'rel', axis=1, tiled=True)  16.3 us
    all_to_all x5, waiting for transfers between devices, swap(): return lax.all_to_all(x, axis, split_axis=0, concat_axis=0, tiled=True)  15.6 us
    reduce_sum x1, other arithmetic, per_device(): grad_rows = jnp.sum(spread * coef_t[:, None, :], axis=0).astype(BF).T  12.5 us
    all_gather x1, blocking collectives, per_device(): act = lax.all_gather(act, 'rel', axis=1, tiled=True)  11.1 us
    all_gather x1, blocking collectives, per_device(): meta = lax.all_gather(meta, 'rel').reshape(rel_count, 3, ent_count, cap)  10.5 us
  transfers between devices with their start and end apart: 6, of which 5 were waited for; matrix products, arithmetic and copies ran while one was open for 22% of the time, Pallas kernels for 0%

profile of v1, /device:TPU:25, one launch (start us, length us, event | category | flops | bytes accessed | tf_op | source)
XLA Modules:
  0.0 227.8 jit_solution(15646126451064702323)
XLA Ops:
  0.6 0.0 copy-start
  0.7 1.8 fusion.33
  2.5 2.1 fusion.32
  4.6 0.7 compare_select_fusion.7
  5.3 0.8 add_add_fusion.1
  6.0 4.5 %compare_select_fusion.1 = (s32[512,1]{0,1:T(1,128)S(1)}, s32[512,1]{0,1:T(1,128)S(1)}) fusion(s32[]{:T(128)} %bitcast.31, s32[]{:T(128)} %bitcast.32, s32[]{:T(128)} %bitcast.33, s32[]{:T(128)} %bitcast.34, s32[]{:T(128)} %bitcast.35, s32[]{:T(128)} %bitcast.37, s32[]{:T(128)} %bitcast.36, s32[512,1]{0,1:T(1,128)S(1)} %bitcast.106, s32[512,1]{0,1:T(1,128)S(1)} %bitcast.105), kind=kLoop, calls=%fused_computation.66 | loop fusion | flops 7168 | bytes 8220 | tf_op jit(solution)/shard_map/jit(_take)/gather | solution.py:45
  10.5 0.2 compare_reduce_fusion.24
  10.7 0.7 broadcast_subtract_fusion
  11.4 3.6 %gather_fusion = s32[512]{0:T(512)S(1)} fusion(s32[250]{0:T(256)} %param.16, s32[1024]{0:T(1024)S(1)} %pad_clamp_fusion), kind=kCustom, calls=%fused_computation | custom fusion | bytes 6144 | tf_op jit(solution)/shard_map/gather | solution.py:49
  15.0 16.4 %fusion.23 = s32[512]{0:T(512)S(1)} fusion(s32[512]{0:T(512)} %param.19, pred[512]{0:T(512)(128)(4,1)S(1)} %get-tuple-element.51, pred[512]{0:T(512)(128)(4,1)S(1)} %get-tuple-element.50, pred[512]{0:T(512)(128)(4,1)S(1)} %get-tuple-element.49, pred[512]{0:T(512)(128)(4,1)S(1)} %get-tuple-element.48, pred[512]{0:T(512)(128)(4,1)S(1)} %get-tuple-element.47, ...), kind=kLoop, calls=%fused_computation.85 | loop fusion | flops 25600 | bytes 21108 | tf_op jit(solution)/shard_map/jit(_where)/select_n | solution.py:48
  31.4 10.5 %all-gather.1 = s32[4,3,512]{2,1,0:T(4,128)S(1)} all-gather(s32[1,3,512]{2,1,0:T(4,128)S(1)} %add_bitcast_fusion), channel_id=2, replica_groups=mesh['rel'=4,'ent'=32] {'rel'}, dimensions={0}, use_global_device_ids=true | all-gather | bytes 30720 | tf_op jit(solution)/shard_map/all_gather | solution.py:51
  41.9 0.1 reshape.134
  42.0 0.1 copy.30
  42.1 0.7 reshape.365
  42.9 10.3 %all-to-all-start = ((s32[32,1,128]{2,1,0:T(1,128)}), s32[32,1,128]{2,1,0:T(1,128)S(1)}, u32[]{:S(2)}, u32[]{:S(2)}) async-start(s32[32,1,128]{2,1,0:T(1,128)} %reshape.365), calls=%async_computation | async-start | bytes 32768 | tf_op jit(solution)/shard_map/all_to_all | solution.py:17
  53.2 0.1 eq.56
  53.3 0.0 copy-done
  53.3 2.1 fusion.6
  55.4 2.8 %all-to-all-done = s32[32,1,128]{2,1,0:T(1,128)S(1)} async-done(((s32[32,1,128]{2,1,0:T(1,128)}), s32[32,1,128]{2,1,0:T(1,128)S(1)}, u32[]{:S(2)}, u32[]{:S(2)}) %all-to-all-start) | async-done | bytes 16416 | tf_op jit(solution)/shard_map/all_to_all | solution.py:17
  58.2 6.1 %all-to-all-start.1 = ((bf16[32,64,128]{2,1,0:T(8,128)(2,1)}), bf16[32,64,128]{2,1,0:T(8,128)(2,1)S(1)}, u32[]{:S(2)}, u32[]{:S(2)}) async-start(bf16[32,64,128]{2,1,0:T(8,128)(2,1)} %bitcast.44), calls=%async_computation.1 | async-start | bytes 1048576 | tf_op jit(solution)/shard_map/all_to_all | solution.py:17
  64.3 0.0 copy-start.4
  64.3 4.6 %constant_dynamic-slice_fusion.1 = bf16[32,128,512]{2,1,0:T(8,128)(2,1)} fusion(bf16[32,512,512]{2,1,0:T(8,128)(2,1)} %bitcast.98, s32[]{:T(128)S(6)} %select_n.47), kind=kLoop, calls=%fused_computation.95 | loop fusion | bytes 8388612 | tf_op jit(solution)/shard_map/dynamic_slice | solution.py:75
  68.9 0.5 broadcast.362
  69.5 0.7 reduce.52
  70.1 0.1 reshape.366
  70.3 0.1 eq.48
  70.4 0.1 eq.52
  70.5 0.0 copy-done.4
  70.5 2.9 %fusion.7 = f32[32,2048]{1,0:T(8,128)S(1)} fusion(f32[1000,32]{0,1:T(8,128)S(1)} %copy-done.4, s32[2048]{0:T(1024)S(1)} %eq.52), kind=kOutput, calls=%fused_computation.18 | convolution fusion | flops 788480000 | bytes 398336 | tf_op jit(solution)/shard_map/dot_general | solution.py:11
  73.5 0.4 all-to-all-done.1
  73.9 0.1 bitcast_convert_fusion
  74.0 0.3 copy.32
  74.4 6.8 %multiply_convert_fusion = bf16[32,128,2048]{2,1,0:T(8,128)(2,1)} fusion(f32[128,2048]{1,0:T(8,128)S(1)} %bitcast.93, f32[32,2048]{1,0:T(8,128)S(1)} %fusion.7), kind=kLoop, calls=%fused_computation.2 | loop fusion | flops 16777216 | bytes 18087936 | tf_op jit(solution)/shard_map/convert_element_type | solution.py:72
  81.2 13.9 %convolution_convert_fusion = bf16[512,4096]{1,0:T(8,128)(2,1)} fusion(bf16[4096,2048]{1,0:T(8,128)(2,1)} %bitcast.92, s32[2048]{0:T(1024)S(1)} %eq.48), kind=kOutput, calls=%fused_computation.6 | convolution fusion | flops 8593080320 | bytes 20979712 | tf_op jit(solution)/shard_map/dot_general | solution.py:11
  95.1 5.5 %convolution_convert_fusion.3 = bf16[512,512]{0,1:T(8,128)(2,1)} fusion(bf16[512,4096]{1,0:T(8,128)(2,1)} %convolution_convert_fusion, bf16[4096,512]{1,0:T(8,128)(2,1)S(1)} %bitcast.95), kind=kOutput, calls=%fused_computation.23 | convolution fusion | flops 2147745792 | bytes 8912896 | tf_op jit(solution)/shard_map/dot_general | solution.py:11
  100.6 3.8 %all-to-all-start.2 = ((bf16[4,512,128]{1,2,0:T(8,128)(2,1)}), bf16[4,512,128]{1,2,0:T(8,128)(2,1)S(1)}, u32[]{:S(2)}, u32[]{:S(2)}) async-start(bf16[4,512,128]{1,2,0:T(8,128)(2,1)} %bitcast.51), calls=%async_computation.2 | async-start | bytes 1048576 | tf_op jit(solution)/shard_map/all_to_all | solution.py:17
  104.4 0.9 constant_dynamic-slice_fusion
  105.3 0.1 copy.36
  105.4 0.5 convert_reduce_fusion.1
  106.0 7.5 %all-to-all-done.2 = bf16[4,512,128]{1,2,0:T(8,128)(2,1)S(1)} async-done(((bf16[4,512,128]{1,2,0:T(8,128)(2,1)}), bf16[4,512,128]{1,2,0:T(8,128)(2,1)S(1)}, u32[]{:S(2)}, u32[]{:S(2)}) %all-to-all-start.2) | async-done | bytes 524320 | tf_op jit(solution)/shard_map/all_to_all | solution.py:17
  113.5 0.1 convert_reduce_fusion.2
  113.5 0.4 multiply_convert_fusion.6
  114.0 10.5 %all_gather.18 = bf16[512,512]{0,1:T(8,128)(2,1)S(1)} all-gather(bf16[512,128]{0,1:T(8,128)(2,1)S(1)} %get-tuple-element.54), channel_id=1, replica_groups=mesh['rel'=4,'ent'=32] {'rel'}, dimensions={1}, use_global_device_ids=true | all-gather | bytes 655360 | tf_op jit(solution)/shard_map/all_gather | solution.py:89
  124.5 6.6 %convolution_convert_fusion.1 = bf16[4096,512]{1,0:T(8,128)(2,1)} fusion(bf16[512,4096]{1,0:T(8,128)(2,1)} %convolution_convert_fusion, bf16[512,512]{0,1:T(8,128)(2,1)S(1)} %all_gather.18, f32[512]{0:T(512)S(1)} %maximum_divide_fusion), kind=kOutput, calls=%fused_computation.7 | convolution fusion | flops 2150367232 | bytes 8914944 | tf_op jit(solution)/shard_map/dot_general | solution.py:11
  131.1 11.0 %all-to-all-start.4 = ((bf16[32,128,512]{2,1,0:T(8,128)(2,1)}), bf16[32,128,512]{2,1,0:T(8,128)(2,1)}, u32[]{:S(2)}, u32[]{:S(2)}) async-start(bf16[32,128,512]{2,1,0:T(8,128)(2,1)} %bitcast.96), calls=%async_computation.4 | async-start | bytes 8388608 | tf_op jit(solution)/shard_map/all_to_all | solution.py:17
  142.1 11.1 %all_gather.17 = bf16[512,512]{0,1:T(8,128)(2,1)S(1)} all-gather(bf16[512,128]{0,1:T(8,128)(2,1)S(1)} %get-tuple-element.55), channel_id=1, replica_groups=mesh['rel'=4,'ent'=32] {'rel'}, dimensions={1}, use_global_device_ids=true | all-gather | bytes 655360 | tf_op jit(solution)/shard_map/all_gather | solution.py:88
  153.2 1.0 copy.35
  154.2 4.5 %convolution_convert_fusion.2.clone.5 = bf16[4096,512]{1,0:T(8,128)(2,1)S(1)} fusion(bf16[4096,512]{1,0:T(8,128)(2,1)} %bitcast.94, bf16[512,512]{0,1:T(8,128)(2,1)S(1)} %all_gather.18, f32[512]{0:T(512)S(1)} %maximum_divide_fusion), kind=kOutput, calls=%fused_computation.8.clone.clone.clone.2 | convolution fusion | flops 2150367232 | bytes 8914944 | tf_op jit(solution)/shard_map/dot_general | solution.py:11
  158.8 14.6 %fusion.3 = f32[4096,2048]{1,0:T(8,128)} fusion(s32[2048]{0:T(1024)S(1)} %eq.48, bf16[4096,512]{1,0:T(8,128)(2,1)S(1)} %convolution_convert_fusion.2.clone.5), kind=kOutput, calls=%fused_computation.14 | convolution fusion | flops 8590983168 | bytes 37756928 | tf_op jit(solution)/shard_map/dot_general | solution.py:11
  173.3 12.5 %multiply_reduce_fusion = bf16[128,2048]{1,0:T(8,128)(2,1)S(1)} fusion(f32[32,128,2048]{2,1,0:T(8,128)} %bitcast.91, f32[32,2048]{1,0:T(8,128)S(1)} %fusion.7), kind=kLoop, calls=%fused_computation.1 | loop fusion | flops 16515072 | bytes 34340864 | tf_op jit(solution)/shard_map/reduce_sum | solution.py:105
  185.8 1.0 copy.34
  186.8 3.6 %all-to-all-done.4 = bf16[32,128,512]{2,1,0:T(8,128)(2,1)} async-done(((bf16[32,128,512]{2,1,0:T(8,128)(2,1)}), bf16[32,128,512]{2,1,0:T(8,128)(2,1)}, u32[]{:S(2)}, u32[]{:S(2)}) %all-to-all-start.4) | async-done | bytes 4194336 | tf_op jit(solution)/shard_map/all_to_all | solution.py:17
  190.5 9.1 %all-to-all-start.3 = ((bf16[32,64,128]{2,1,0:T(8,128)(2,1)}), bf16[32,64,128]{2,1,0:T(8,128)(2,1)S(1)}, u32[]{:S(2)}, u32[]{:S(2)}) async-start(bf16[32,64,128]{2,1,0:T(8,128)(2,1)} %bitcast.54), calls=%async_computation.3 | async-start | bytes 1048576 | tf_op jit(solution)/shard_map/all_to_all | solution.py:17
  199.5 0.0 copy-start.1
  199.6 0.3 fusion.15
  199.9 2.8 %convert_reduce_fusion = f32[128,512]{1,0:T(8,128)S(1)} fusion(bf16[32,128,512]{2,1,0:T(8,128)(2,1)} %all-to-all-done.4), kind=kLoop, calls=%fused_computation.3 | loop fusion | flops 4128768 | bytes 4456448 | tf_op jit(solution)/shard_map/reduce_sum | solution.py:94
  202.7 5.3 %collective-permute-start = (f32[128,512]{1,0:T(8,128)S(1)}, f32[128,512]{1,0:T(8,128)S(1)}, u32[]{:S(2)}, u32[]{:S(2)}) collective-permute-start(f32[128,512]{1,0:T(8,128)S(1)} %convert_reduce_fusion), channel_id=1, source_target_pairs={{0,0},{1,4},{2,8},{3,12},{4,16},{5,20},{6,24},{7,28},{8,32},{9,36}... | collective-permute-start | bytes 786440 | tf_op jit(solution)/shard_map/ppermute | solution.py:101
  208.0 1.1 all-to-all-done.3
  209.1 0.9 fusion.14
  210.0 16.3 %all_gather.19 = bf16[512,512]{1,0:T(8,128)(2,1)S(1)} all-gather(bf16[512,128]{1,0:T(8,128)(2,1)S(1)} %fusion.14), channel_id=1, replica_groups=mesh['rel'=4,'ent'=32] {'rel'}, dimensions={1}, use_global_device_ids=true | all-gather | bytes 655360 | tf_op jit(solution)/shard_map/all_gather | solution.py:111
  226.3 0.0 collective-permute-done
  226.3 0.8 copy.39
  227.1 0.7 copy.40
  227.8 0.0 copy-done.1
  (13 shorter events, 0.1 us)
Async XLA Ops:
  0.6 52.7 %copy-start = (bf16[512,512]{1,0:T(8,128)(2,1)S(1)}, bf16[512,512]{1,0:T(8,128)(2,1)}, u32[]{:S(2)}) copy-start(bf16[512,512]{1,0:T(8,128)(2,1)} %param.12) | copy-start | bytes 1572868
  42.9 15.4 %all-to-all-start = ((s32[32,1,128]{2,1,0:T(1,128)}), s32[32,1,128]{2,1,0:T(1,128)S(1)}, u32[]{:S(2)}, u32[]{:S(2)}) async-start(s32[32,1,128]{2,1,0:T(1,128)} %reshape.365), calls=%async_computation | async-start | bytes 32768 | tf_op jit(solution)/shard_map/all_to_all | solution.py:17
  58.2 15.7 %all-to-all-start.1 = ((bf16[32,64,128]{2,1,0:T(8,128)(2,1)}), bf16[32,64,128]{2,1,0:T(8,128)(2,1)S(1)}, u32[]{:S(2)}, u32[]{:S(2)}) async-start(bf16[32,64,128]{2,1,0:T(8,128)(2,1)} %bitcast.44), calls=%async_computation.1 | async-start | bytes 1048576 | tf_op jit(solution)/shard_map/all_to_all | solution.py:17
  64.3 6.2 %copy-start.4 = (f32[1000,32]{0,1:T(8,128)S(1)}, f32[1000,32]{0,1:T(8,128)}, u32[]{:S(2)}) copy-start(f32[1000,32]{0,1:T(8,128)} %param.15) | copy-start | bytes 384004
  81.2 13.9 %copy-start.2 = (bf16[32,128,512]{2,1,0:T(8,128)(2,1)S(1)}, bf16[32,128,512]{2,1,0:T(8,128)(2,1)}, u32[]{:S(2)}) copy-start(bf16[32,128,512]{2,1,0:T(8,128)(2,1)} %constant_dynamic-slice_fusion.1) | copy-start | bytes 12582916
  95.1 18.4 %copy-start.3 = (bf16[512,512]{1,0:T(8,128)(2,1)S(1)}, bf16[512,512]{1,0:T(8,128)(2,1)}, u32[]{:S(2)}) copy-start(bf16[512,512]{1,0:T(8,128)(2,1)} %param.13) | copy-start | bytes 1572868
  100.6 12.9 %all-to-all-start.2 = ((bf16[4,512,128]{1,2,0:T(8,128)(2,1)}), bf16[4,512,128]{1,2,0:T(8,128)(2,1)S(1)}, u32[]{:S(2)}, u32[]{:S(2)}) async-start(bf16[4,512,128]{1,2,0:T(8,128)(2,1)} %bitcast.51), calls=%async_computation.2 | async-start | bytes 1048576 | tf_op jit(solution)/shard_map/all_to_all | solution.py:17
  131.1 59.4 %all-to-all-start.4 = ((bf16[32,128,512]{2,1,0:T(8,128)(2,1)}), bf16[32,128,512]{2,1,0:T(8,128)(2,1)}, u32[]{:S(2)}, u32[]{:S(2)}) async-start(bf16[32,128,512]{2,1,0:T(8,128)(2,1)} %bitcast.96), calls=%async_computation.4 | async-start | bytes 8388608 | tf_op jit(solution)/shard_map/all_to_all | solution.py:17
  190.5 18.7 %all-to-all-start.3 = ((bf16[32,64,128]{2,1,0:T(8,128)(2,1)}), bf16[32,64,128]{2,1,0:T(8,128)(2,1)S(1)}, u32[]{:S(2)}, u32[]{:S(2)}) async-start(bf16[32,64,128]{2,1,0:T(8,128)(2,1)} %bitcast.54), calls=%async_computation.3 | async-start | bytes 1048576 | tf_op jit(solution)/shard_map/all_to_all | solution.py:17
  199.5 28.3 %copy-start.1 = (bf16[512,512]{1,0:T(8,128)(2,1)S(1)}, bf16[512,512]{1,0:T(8,128)(2,1)}, u32[]{:S(2)}) copy-start(bf16[512,512]{1,0:T(8,128)(2,1)} %param.12) | copy-start | bytes 1572868
  202.7 23.6 %collective-permute-start = (f32[128,512]{1,0:T(8,128)S(1)}, f32[128,512]{1,0:T(8,128)S(1)}, u32[]{:S(2)}, u32[]{:S(2)}) collective-permute-start(f32[128,512]{1,0:T(8,128)S(1)} %convert_reduce_fusion), channel_id=1, source_target_pairs={{0,0},{1,4},{2,8},{3,12},{4,16},{5,20},{6,24},{7,28},{8,32},{9,36}... | collective-permute-start | bytes 786440 | tf_op jit(solution)/shard_map/ppermute | solution.py:101

commit v2 on v1

v2 whole, which is shorter than its diff:
```python
import functools

import jax
import jax.numpy as jnp
from jax import lax
from jax.experimental import pallas as pl
from jax.experimental.pallas import tpu as pltpu
from jax.sharding import PartitionSpec as P

BF = jnp.bfloat16
F32 = jnp.float32
I32 = jnp.int32
MIB = 1 << 20


def dot(a, b, dims=((1,), (0,))):
    return lax.dot_general(a, b, (dims, ((), ())), preferred_element_type=F32)


def swap(x, axis):
    return lax.all_to_all(x, axis, split_axis=0, concat_axis=0, tiled=True)


def one_hot(count, row):
    ids = lax.broadcasted_iota(I32, (count, row.shape[1]), 0)
    return (ids == row).astype(F32).astype(BF)


def split3(x):
    hi = x.astype(BF)
    rest = x - hi.astype(F32)
    mid = rest.astype(BF)
    lo = (rest - mid.astype(F32)).astype(BF)
    return hi, mid, lo


def forward_kernel(
    group,
    dst_ref,
    rel_ref,
    rows_ref,
    coef_ref,
    basis_hbm,
    part_ref,
    agg_ref,
    inv_ref,
    coef_t_ref,
    basis,
    table,
    pick,
    rows_t,
    acc,
    sem,
):
    q = lax.axis_index("rel")
    bases, part, width = basis.shape
    rels = coef_ref.shape[0]
    n_ent = pick.shape[0]
    load = pltpu.make_async_copy(
        basis_hbm.at[:, pl.ds(pl.multiple_of(q * part, part), part), :], basis, sem
    )
    load.start()
    table[...] = jnp.zeros_like(table)
    table[:rels, :bases] = coef_ref[...]
    which = one_hot(table.shape[0], rel_ref[...])
    hi, mid, lo = split3(table[...])
    coef_t = dot(hi, which, ((0,), (0,))) + dot(mid, which, ((0,), (0,)))
    coef_t = coef_t + dot(lo, which, ((0,), (0,)))
    coef_t_ref[...] = coef_t[:bases, :]
    pick[...] = one_hot(n_ent, dst_ref[...])
    degree = dot(pick[...], jnp.ones((pick.shape[1], part), BF))
    inv_ref[...] = 1.0 / jnp.maximum(degree, 1.0)
    rows_t[...] = rows_ref[...].astype(F32).T
    acc[...] = jnp.zeros_like(acc)
    load.wait()

    def step(i, _):
        mixed = jnp.concatenate(
            [
                (rows_t[...] * coef_t_ref[pl.ds(i * group + g, 1), :]).astype(BF)
                for g in range(group)
            ],
            axis=0,
        )
        agg = dot(pick[...], mixed, ((1,), (1,)))
        agg_b = agg.astype(BF)
        weights = basis[pl.ds(i * group, group)].reshape(group * part, width)
        acc[...] += dot(agg_b, weights)
        agg_ref[pl.ds(i * group, group)] = agg.T.astype(BF).reshape(group, part, n_ent)
        return 0

    lax.fori_loop(0, bases // group, step, 0)
    for r in range(width // part):
        part_ref[r] = acc[:, r * part : (r + 1) * part].astype(BF)


def forward(dst, rel, rows, coeffs, basis_mats, n_ent):
    all_slots, part = rows.shape
    rels, bases = coeffs.shape
    width = basis_mats.shape[1]
    vm = pl.BlockSpec(memory_space=pltpu.VMEM)
    return pl.pallas_call(
        functools.partial(forward_kernel, 2),
        out_shape=(
            jax.ShapeDtypeStruct((width // part, n_ent, part), BF),
            jax.ShapeDtypeStruct((bases, part, n_ent), BF),
            jax.ShapeDtypeStruct((n_ent, part), F32),
            jax.ShapeDtypeStruct((bases, all_slots), F32),
        ),
        in_specs=[vm, vm, vm, vm, pl.BlockSpec(memory_space=pl.ANY)],
        out_specs=(vm, vm, vm, vm),
        scratch_shapes=[
            pltpu.VMEM((bases, part, width), BF),
            pltpu.VMEM((1024, 128), F32),
            pltpu.VMEM((n_ent, all_slots), BF),
            pltpu.VMEM((part, all_slots), F32),
            pltpu.VMEM((n_ent, width), F32),
            pltpu.SemaphoreType.DMA,
        ],
        compiler_params=pltpu.CompilerParams(vmem_limit_bytes=56 * MIB),
    )(dst, rel, rows, coeffs, basis_mats.reshape(bases, width, width))


def terms_kernel(agg_ref, scaled_ref, out_ref):
    group, part, n_ent = agg_ref.shape
    terms = dot(agg_ref[...].reshape(group * part, n_ent), scaled_ref[...])
    out_ref[...] = terms.astype(BF).reshape(out_ref.shape)


def basis_terms(agg, scaled):
    bases, part, n_ent = agg.shape
    width = scaled.shape[1]
    group = 8
    return pl.pallas_call(
        terms_kernel,
        out_shape=jax.ShapeDtypeStruct((bases, part, width), BF),
        grid=(bases // group,),
        in_specs=[
            pl.BlockSpec((group, part, n_ent), lambda i: (i, 0, 0)),
            pl.BlockSpec((n_ent, width), lambda i: (0, 0)),
        ],
        out_specs=pl.BlockSpec((group, part, width), lambda i: (i, 0, 0)),
        compiler_params=pltpu.CompilerParams(vmem_limit_bytes=32 * MIB),
    )(agg, scaled)


def backward_kernel(
    group, scaled_ref, dst_ref, coef_t_ref, basis_hbm, out_ref, basis, pick, acc, sem
):
    q = lax.axis_index("rel")
    bases, part, width = basis.shape
    load = pltpu.make_async_copy(
        basis_hbm.at[:, pl.ds(pl.multiple_of(q * part, part), part), :], basis, sem
    )
    load.start()
    pick[...] = one_hot(pick.shape[0], dst_ref[...])
    acc[...] = jnp.zeros_like(acc)
    load.wait()

    def step(i, _):
        weights = basis[pl.ds(i * group, group)].reshape(group * part, width)
        back = dot(weights, scaled_ref[...], ((1,), (1,))).astype(BF)
        spread = dot(back, pick[...])
        total = acc[...]
        for g in range(group):
            total += (
                spread[g * part : (g + 1) * part] * coef_t_ref[pl.ds(i * group + g, 1), :]
            )
        acc[...] = total
        return 0

    lax.fori_loop(0, bases // group, step, 0)
    out_ref[...] = acc[...].T.astype(BF)


def backward(scaled, dst, coef_t, basis_mats):
    bases, all_slots = coef_t.shape
    n_ent, width = scaled.shape
    part = 128
    vm = pl.BlockSpec(memory_space=pltpu.VMEM)
    return pl.pallas_call(
        functools.partial(backward_kernel, 4),
        out_shape=jax.ShapeDtypeStruct((all_slots, part), BF),
        in_specs=[vm, vm, vm, pl.BlockSpec(memory_space=pl.ANY)],
        out_specs=vm,
        scratch_shapes=[
            pltpu.VMEM((bases, part, width), BF),
            pltpu.VMEM((n_ent, all_slots), BF),
            pltpu.VMEM((part, all_slots), F32),
            pltpu.SemaphoreType.DMA,
        ],
        compiler_params=pltpu.CompilerParams(vmem_limit_bytes=56 * MIB),
    )(scaled, dst, coef_t, basis_mats.reshape(bases, width, width))


def per_device(
    features,
    w_self,
    basis_mats,
    basis_coeffs,
    group_rels,
    rel_local,
    edge_src,
    edge_dst,
    block_counts,
    cotangent,
):
    n_ent, width = features.shape
    ent_count = lax.axis_size("ent")
    rel_count = lax.axis_size("rel")
    slots = rel_local.shape[0]
    cap = slots // ent_count
    bases = basis_coeffs.shape[1]
    part = width // rel_count
    q = lax.axis_index("rel")
    s = lax.axis_index("ent")
    all_slots = slots * rel_count

    shape = (ent_count, cap)
    live = lax.broadcasted_iota(I32, shape, 1) < block_counts.reshape(ent_count, 1)
    src_own = edge_src.reshape(shape) - s * n_ent
    base = lax.broadcasted_iota(I32, shape, 0) * n_ent
    dst_own = jnp.where(live, edge_dst.reshape(shape) - base, n_ent)
    ids = jnp.arange(group_rels.shape[0], dtype=I32)
    rel_own = jnp.sum(
        jnp.where(rel_local[:, None] == ids[None, :], group_rels[None, :], 0), axis=1
    ).reshape(shape)
    meta = jnp.stack([src_own, dst_own, rel_own])
    meta = lax.all_gather(meta, "rel")
    meta = meta.transpose(2, 1, 0, 3)
    src = meta[:, 0].reshape(1, all_slots)
    arrived = swap(meta[:, 1:], "ent")
    dst = arrived[:, 0].reshape(1, all_slots)
    rel = arrived[:, 1].reshape(1, all_slots)

    pick_src = (jnp.arange(n_ent, dtype=I32)[:, None] == src).astype(BF)
    feat_part = lax.dynamic_slice_in_dim(features, q * part, part, 1)
    rows = dot(pick_src, feat_part, ((0,), (0,))).astype(BF)
    rows = swap(rows.reshape(ent_count, rel_count * cap, part), "ent").reshape(all_slots, part)

    partial, agg, inverse, coef_t = forward(dst, rel, rows, basis_coeffs, basis_mats, n_ent)
    partial = swap(partial, "rel")
    sums = jnp.sum(partial.astype(F32), axis=0)

    w_part = lax.dynamic_slice_in_dim(w_self, q * part, part, 1)
    cot = lax.dynamic_slice_in_dim(cotangent, q * part, part, 1).astype(F32)
    pre = dot(features, w_part) + sums * inverse
    sig = jax.nn.sigmoid(pre)
    act = (pre * sig).astype(BF)
    grad_pre = (cot * (sig * (1.0 + pre * (1.0 - sig)))).astype(BF)
    both = lax.all_gather(jnp.stack([act, grad_pre]), "rel")
    act = both[:, 0].transpose(1, 0, 2).reshape(n_ent, width)
    grad_pre = both[:, 1].transpose(1, 0, 2).reshape(n_ent, width)
    scaled = (grad_pre.astype(F32) * inverse[:, :1]).astype(BF)

    terms = swap(basis_terms(agg, scaled), "ent")
    block = jnp.sum(terms.astype(F32), axis=0)
    per_rel = bases // rel_count
    routes = [
        (r * ent_count + b, (b // per_rel) * ent_count + (b % per_rel) * rel_count + r)
        for r in range(rel_count)
        for b in range(bases)
    ]
    grad_basis = lax.ppermute(block, ("rel", "ent"), routes)

    grad_rows = backward(scaled, dst, coef_t, basis_mats)
    grad_rows = swap(grad_rows.reshape(ent_count, rel_count * cap, part), "ent")
    w_rows = lax.dynamic_slice_in_dim(w_self, q * part, part, 0)
    grad_part = dot(grad_pre, w_rows, ((1,), (1,))) + dot(
        pick_src, grad_rows.reshape(all_slots, part)
    )
    grad_features = lax.all_gather(grad_part.astype(BF), "rel", axis=1, tiled=True)
    return act, grad_features, grad_basis


def solution(mesh):
    placed = (
        P("ent", None),
        P(),
        P(),
        P(),
        P("rel"),
        P(("rel", "ent")),
        P(("rel", "ent")),
        P(("rel", "ent")),
        P("rel", "ent", None),
        P("ent", None),
    )
    return jax.shard_map(
        per_device,
        mesh=mesh,
        in_specs=placed,
        out_specs=(P("ent", None), P("ent", None), P(("rel", "ent"), None)),
        check_vma=False,
    )
```

time: 230 us -> 228 us (level)
  matrix products: 51.8 us -> 4.6 us
  waiting for transfers between devices: 15.6 us -> 61 us
  Pallas kernels: 0 us -> 44.8 us
  other arithmetic: 46.6 us -> 6.87 us
  between operations: 0.91 us -> 14.3 us
  blocking collectives: 48.4 us -> 41.3 us
  starting transfers between devices: 45.6 us -> 39.9 us
  local copies, waits for them, and re-layouts: 19 us -> 13.3 us
    dot_general x10 -> x4, matrix products: 51.8 us -> 4.6 us  [dot(): return lax.dot_general(a, b, (dims, ((), ())), preferred_element_type=F32)]
    pallas_call x0 -> x3, Pallas kernels: none -> 44.8 us  [the longest x1 25 us: forward(): pl.pallas_call(functools.partial(forward_kernel, 2), out_shape=(jax.Shape...]
    all_to_all x5 -> x4, waiting for transfers between devices: 15.6 us -> 39.2 us  [swap(): return lax.all_to_all(x, axis, split_axis=0, concat_axis=0, tiled=True)]
    all_gather x0 -> x1, waiting for transfers between devices: none -> 21.8 us  [per_device(): both = lax.all_gather(jnp.stack([act, grad_pre]), 'rel')]
    all_gather x3 -> x1, blocking collectives: 32.1 us -> 10.6 us  [per_device(): meta = lax.all_gather(meta, 'rel')]
    select_n x2 -> x1, other arithmetic: 17 us -> 0.73 us  [per_device(): dst_own = jnp.where(live, edge_dst.reshape(shape) - base, n_ent)]
    all_to_all x0 -> x1, blocking collectives: none -> 13.1 us  [swap(): return lax.all_to_all(x, axis, split_axis=0, concat_axis=0, tiled=True)]
    reduce_sum x3 -> x2, other arithmetic: 15.8 us -> 3.79 us  [the longest x1 2.8 us: per_device(): block = jnp.sum(terms.astype(F32), axis=0)]
  transfers between devices with their start and end apart: 6 -> 6, of which waited for: 5 -> 5; matrix products, arithmetic and copies ran while one was open for 22% -> 5% of each run, Pallas kernels for 0% -> 7%
where the time goes in v2:
time: 228 us; the launch traced here: 226 us
  waiting for transfers between devices  61 us (27%)
  Pallas kernels  44.8 us (20%)
  blocking collectives  41.3 us (18%)
  starting transfers between devices  39.9 us (18%)
  between operations  14.3 us (6%)
  local copies, waits for them, and re-layouts  13.3 us (6%)
  other arithmetic  6.87 us (3%)
  matrix products  4.6 us (2%)
    all_to_all x4, waiting for transfers between devices, swap(): return lax.all_to_all(x, axis, split_axis=0, concat_axis=0, tiled=True)  39.2 us
    all_to_all x4, starting transfers between devices, swap(): return lax.all_to_all(x, axis, split_axis=0, concat_axis=0, tiled=True)  34.1 us
    pallas_call x1, Pallas kernels, forward(): pl.pallas_call(functools.partial(forward_kernel, 2), out_shape=(jax.Shape...  25 us
    all_gather x1, waiting for transfers between devices, per_device(): both = lax.all_gather(jnp.stack([act, grad_pre]), 'rel')  21.8 us
    all_gather x1, blocking collectives, per_device(): lax.all_gather(grad_part.astype(BF), 'rel', axis=1, tiled=True)  17.5 us
    pallas_call x1, Pallas kernels, backward(): pl.pallas_call(functools.partial(backward_kernel, 4), out_shape=jax.Shape...  16.9 us
    all_to_all x1, blocking collectives, swap(): return lax.all_to_all(x, axis, split_axis=0, concat_axis=0, tiled=True)  13.1 us
    all_gather x1, blocking collectives, per_device(): meta = lax.all_gather(meta, 'rel')  10.6 us
  transfers between devices with their start and end apart: 6, of which 5 were waited for; matrix products, arithmetic and copies ran while one was open for 5% of the time, Pallas kernels for 7%

profile of v2, /device:TPU:25, one launch (start us, length us, event | category | flops | bytes accessed | tf_op | source)
XLA Modules:
  0.0 226.0 jit_solution(5505248825867816418)
XLA Ops:
  7.2 0.0 copy-start
  7.2 0.0 copy-start.6
  7.2 1.0 select_reduce_fusion
  8.2 0.1 stack_reshape.3
  8.3 0.8 reshape.113
  9.0 0.7 broadcast_subtract_fusion
  9.7 0.1 sub.31
  9.8 0.7 subtract_select_fusion
  10.6 0.1 copy.33
  10.6 10.6 %all-gather = s32[12,32,16]{1,2,0:T(8,128)S(1)} all-gather(s32[3,32,16]{1,2,0:T(8,128)S(1)} %copy.33), channel_id=2, replica_groups=mesh['rel'=4,'ent'=32] {'rel'}, dimensions={0}, use_global_device_ids=true | all-gather | bytes 30720 | tf_op jit(solution)/shard_map/all_gather | solution.py:229
  21.3 0.1 copy.34
  21.4 0.8 reshape.136
  22.2 10.2 %all-to-all-start = ((s32[32,1,128]{2,1,0:T(1,128)}), s32[32,1,128]{2,1,0:T(1,128)S(1)}, u32[]{:S(2)}, u32[]{:S(2)}) async-start(s32[32,1,128]{2,1,0:T(1,128)} %reshape.136), calls=%async_computation | async-start | bytes 32768 | tf_op jit(solution)/shard_map/all_to_all | solution.py:21
  32.4 0.1 copy.35
  32.5 0.1 eq.32
  32.6 0.0 copy-done
  32.6 2.1 fusion.2
  34.7 2.8 %all-to-all-done = s32[32,1,128]{2,1,0:T(1,128)S(1)} async-done(((s32[32,1,128]{2,1,0:T(1,128)}), s32[32,1,128]{2,1,0:T(1,128)S(1)}, u32[]{:S(2)}, u32[]{:S(2)}) %all-to-all-start) | async-done | bytes 16416 | tf_op jit(solution)/shard_map/all_to_all | solution.py:21
  37.5 6.1 %all-to-all-start.1 = ((bf16[32,64,128]{2,1,0:T(8,128)(2,1)}), bf16[32,64,128]{2,1,0:T(8,128)(2,1)S(1)}, u32[]{:S(2)}, u32[]{:S(2)}) async-start(bf16[32,64,128]{2,1,0:T(8,128)(2,1)} %bitcast.5), calls=%async_computation.1 | async-start | bytes 1048576 | tf_op jit(solution)/shard_map/all_to_all | solution.py:21
  43.6 0.0 all-gather.4.cloned.1.call-start
  43.6 0.0 copy-done.6
  43.6 1.0 copy.36.coef_ref
  44.6 0.5 broadcast.67
  45.1 0.7 reduce.10
  45.8 0.2 reshape.137
  46.0 0.4 slice_reduce_fusion.1
  46.4 0.7 reshape_squeeze.7.dst_ref
  47.1 0.7 reshape_squeeze.8.rel_ref
  47.8 5.3 %all-to-all-done.1 = bf16[32,64,128]{2,1,0:T(8,128)(2,1)S(1)} async-done(((bf16[32,64,128]{2,1,0:T(8,128)(2,1)}), bf16[32,64,128]{2,1,0:T(8,128)(2,1)S(1)}, u32[]{:S(2)}, u32[]{:S(2)}) %all-to-all-start.1) | async-done | bytes 524320 | tf_op jit(solution)/shard_map/all_to_all | solution.py:21
  53.1 0.8 copy-done.4
  53.9 25.0 %shard_map.121 = (bf16[4,512,128]{2,1,0:T(8,128)(2,1)}, bf16[32,128,512]{2,1,0:T(8,128)(2,1)}, f32[512,128]{1,0:T(8,128)}, f32[32,2048]{1,0:T(8,128)}) custom-call(s32[1,2048]{1,0:T(1,128)} %reshape_squeeze.7.dst_ref, s32[1,2048]{1,0:T(1,128)} %reshape_squeeze.8.rel_ref, bf16[2048,128]{1,0:T(8,128)(2,1)} %bitcast.46, f32[1000,32]{1,0:T(8,128)} %copy.36.coef_ref, ...), custom_call_target="tpu_custom_call" | custom-call | tf_op jit(solution)/shard_map/pallas_call | solution.py:102
  79.0 0.0 copy-start.5
  79.0 13.1 %all_to_all.25 = bf16[4,512,128]{2,1,0:T(8,128)(2,1)S(1)} all-to-all(bf16[4,512,128]{2,1,0:T(8,128)(2,1)} %get-tuple-element.7), channel_id=1, replica_groups=mesh['rel'=4,'ent'=32] {'rel'}, dimensions={0} | all-to-all | bytes 1048576 | tf_op jit(solution)/shard_map/all_to_all | solution.py:21
  92.1 0.1 convert_reduce_fusion.1
  92.2 0.0 copy-done.7
  92.2 1.4 fusion.14
  93.5 0.7 pad_maximum_fusion
  94.3 0.0 all-gather.4.cloned.1.call-update
  94.3 0.0 copy-done.5
  94.3 0.1 slice_reduce_fusion
  94.4 21.8 %all-gather.4.cloned.1.call-done = bf16[8,512,128]{2,1,0:T(8,128)(2,1)} async-done(((bf16[2,512,128]{2,1,0:T(8,128)(2,1)}), bf16[8,512,128]{2,1,0:T(8,128)(2,1)}) %all-gather.4.cloned.1.call-update) | async-done | bytes 1048592 | tf_op jit(solution)/shard_map/all_gather | solution.py:251
  116.2 1.4 fusion.19
  117.6 0.4 copy.40
  118.0 0.2 multiply_convert_fusion.scaled_ref
  118.2 0.0 copy-start.2
  118.2 0.5 copy-done.3
  118.7 2.8 %shard_map.123 = bf16[32,128,512]{2,1,0:T(8,128)(2,1)S(1)} custom-call(bf16[32,128,512]{2,1,0:T(8,128)(2,1)S(1)} %copy-done.3, bf16[512,512]{1,0:T(8,128)(2,1)S(1)} %multiply_convert_fusion.scaled_ref), custom_call_target="tpu_custom_call" | custom-call | tf_op jit(solution)/shard_map/pallas_call | solution.py:134
  121.6 0.0 copy-done.2
  121.6 0.0 copy-start.1
  121.6 2.0 copy-done.1
  123.5 8.7 %all-to-all-start.4 = ((bf16[32,128,512]{2,1,0:T(8,128)(2,1)}), bf16[32,128,512]{2,1,0:T(8,128)(2,1)}, u32[]{:S(2)}, u32[]{:S(2)}) async-start(bf16[32,128,512]{2,1,0:T(8,128)(2,1)} %copy-done.1), calls=%async_computation.4 | async-start | bytes 8388608 | tf_op jit(solution)/shard_map/all_to_all | solution.py:21
  132.2 0.9 copy.49
  133.1 16.9 %shard_map.122 = bf16[2048,128]{1,0:T(8,128)(2,1)} custom-call(bf16[512,512]{1,0:T(8,128)(2,1)} %copy-done.2, s32[1,2048]{1,0:T(1,128)} %reshape_squeeze.7.dst_ref, f32[32,2048]{1,0:T(8,128)} %get-tuple-element.9.coef_t_ref, bf16[32,512,512]{2,1,0:T(8,128)(2,1)} %bitcast.43), custom_call_target="tpu_custom_call" | custom-call | tf_op jit(solution)/shard_map/pallas_call | solution.py:181
  150.0 30.4 %all-to-all-done.4 = bf16[32,128,512]{2,1,0:T(8,128)(2,1)} async-done(((bf16[32,128,512]{2,1,0:T(8,128)(2,1)}), bf16[32,128,512]{2,1,0:T(8,128)(2,1)}, u32[]{:S(2)}, u32[]{:S(2)}) %all-to-all-start.4) | async-done | bytes 4194336 | tf_op jit(solution)/shard_map/all_to_all | solution.py:21
  180.4 9.2 %all-to-all-start.3 = ((bf16[32,64,128]{2,1,0:T(8,128)(2,1)}), bf16[32,64,128]{2,1,0:T(8,128)(2,1)S(1)}, u32[]{:S(2)}, u32[]{:S(2)}) async-start(bf16[32,64,128]{2,1,0:T(8,128)(2,1)} %bitcast.47), calls=%async_computation.3 | async-start | bytes 1048576 | tf_op jit(solution)/shard_map/all_to_all | solution.py:21
  189.7 0.3 fusion.8
  190.0 2.8 %convert_reduce_fusion = f32[128,512]{1,0:T(8,128)S(1)} fusion(bf16[32,128,512]{2,1,0:T(8,128)(2,1)} %all-to-all-done.4), kind=kLoop, calls=%fused_computation | loop fusion | flops 4128768 | bytes 4456448 | tf_op jit(solution)/shard_map/reduce_sum | solution.py:257
  192.8 5.8 %collective-permute-start = (f32[128,512]{1,0:T(8,128)S(1)}, f32[128,512]{1,0:T(8,128)S(1)}, u32[]{:S(2)}, u32[]{:S(2)}) collective-permute-start(f32[128,512]{1,0:T(8,128)S(1)} %convert_reduce_fusion), channel_id=1, source_target_pairs={{0,0},{1,4},{2,8},{3,12},{4,16},{5,20},{6,24},{7,28},{8,32},{9,36}... | collective-permute-start | bytes 786440 | tf_op jit(solution)/shard_map/ppermute | solution.py:264
  198.5 0.7 all-to-all-done.3
  199.2 0.9 fusion.7
  200.1 17.5 %all_gather.19 = bf16[512,512]{1,0:T(8,128)(2,1)S(1)} all-gather(bf16[512,128]{1,0:T(8,128)(2,1)S(1)} %fusion.7), channel_id=1, replica_groups=mesh['rel'=4,'ent'=32] {'rel'}, dimensions={1}, use_global_device_ids=true | all-gather | bytes 655360 | tf_op jit(solution)/shard_map/all_gather | solution.py:272
  217.6 0.0 collective-permute-done
  217.6 0.8 copy.52
  218.4 0.7 copy.53
  (7 shorter events, 0.0 us)
Async XLA Ops:
  7.2 25.4 %copy-start = (bf16[512,512]{1,0:T(8,128)(2,1)S(1)}, bf16[512,512]{1,0:T(8,128)(2,1)}, u32[]{:S(2)}) copy-start(bf16[512,512]{1,0:T(8,128)(2,1)} %param.10) | copy-start | bytes 1572868
  7.2 36.4 %copy-start.6 = (f32[1000,32]{0,1:T(8,128)S(1)}, f32[1000,32]{0,1:T(8,128)}, u32[]{:S(2)}) copy-start(f32[1000,32]{0,1:T(8,128)} %param.13) | copy-start | bytes 384004
  22.2 15.3 %all-to-all-start = ((s32[32,1,128]{2,1,0:T(1,128)}), s32[32,1,128]{2,1,0:T(1,128)S(1)}, u32[]{:S(2)}, u32[]{:S(2)}) async-start(s32[32,1,128]{2,1,0:T(1,128)} %reshape.136), calls=%async_computation | async-start | bytes 32768 | tf_op jit(solution)/shard_map/all_to_all | solution.py:21
  37.5 15.7 %all-to-all-start.1 = ((bf16[32,64,128]{2,1,0:T(8,128)(2,1)}), bf16[32,64,128]{2,1,0:T(8,128)(2,1)S(1)}, u32[]{:S(2)}, u32[]{:S(2)}) async-start(bf16[32,64,128]{2,1,0:T(8,128)(2,1)} %bitcast.5), calls=%async_computation.1 | async-start | bytes 1048576 | tf_op jit(solution)/shard_map/all_to_all | solution.py:21
  43.6 72.6 %all-gather.4.cloned.1.call-start = ((), (), s32[]{:S(2)}) async-start(), calls=%async_computation.5 | async-start | bytes 1310720 | tf_op jit(solution)/shard_map/all_gather | solution.py:251
  53.1 0.8 copy-start.4
  53.9 38.2 %copy-start.7 = (bf16[512,512]{1,0:T(8,128)(2,1)S(1)}, bf16[512,512]{1,0:T(8,128)(2,1)}, u32[]{:S(2)}) copy-start(bf16[512,512]{1,0:T(8,128)(2,1)} %param.11) | copy-start | bytes 1572868
  79.0 15.3 %copy-start.5 = (f32[512,128]{1,0:T(8,128)S(1)}, f32[512,128]{1,0:T(8,128)}, u32[]{:S(2)}) copy-start(f32[512,128]{1,0:T(8,128)} %get-tuple-element.8) | copy-start | bytes 786436
  116.2 2.5 %copy-start.3 = (bf16[32,128,512]{2,1,0:T(8,128)(2,1)S(1)}, bf16[32,128,512]{2,1,0:T(8,128)(2,1)}, u32[]{:S(2)}) copy-start(bf16[32,128,512]{2,1,0:T(8,128)(2,1)} %get-tuple-element.10.agg_ref) | copy-start | bytes 12582916
  118.2 3.3 %copy-start.2 = (bf16[512,512]{1,0:T(8,128)(2,1)}, bf16[512,512]{1,0:T(8,128)(2,1)S(1)}, u32[]{:S(2)}) copy-start(bf16[512,512]{1,0:T(8,128)(2,1)S(1)} %multiply_convert_fusion.scaled_ref) | copy-start | bytes 1572868
  121.6 2.0 copy-start.1
  123.5 56.9 %all-to-all-start.4 = ((bf16[32,128,512]{2,1,0:T(8,128)(2,1)}), bf16[32,128,512]{2,1,0:T(8,128)(2,1)}, u32[]{:S(2)}, u32[]{:S(2)}) async-start(bf16[32,128,512]{2,1,0:T(8,128)(2,1)} %copy-done.1), calls=%async_computation.4 | async-start | bytes 8388608 | tf_op jit(solution)/shard_map/all_to_all | solution.py:21
  180.4 18.8 %all-to-all-start.3 = ((bf16[32,64,128]{2,1,0:T(8,128)(2,1)}), bf16[32,64,128]{2,1,0:T(8,128)(2,1)S(1)}, u32[]{:S(2)}, u32[]{:S(2)}) async-start(bf16[32,64,128]{2,1,0:T(8,128)(2,1)} %bitcast.47), calls=%async_computation.3 | async-start | bytes 1048576 | tf_op jit(solution)/shard_map/all_to_all | solution.py:21
  192.8 24.9 %collective-permute-start = (f32[128,512]{1,0:T(8,128)S(1)}, f32[128,512]{1,0:T(8,128)S(1)}, u32[]{:S(2)}, u32[]{:S(2)}) collective-permute-start(f32[128,512]{1,0:T(8,128)S(1)} %convert_reduce_fusion), channel_id=1, source_target_pairs={{0,0},{1,4},{2,8},{3,12},{4,16},{5,20},{6,24},{7,28},{8,32},{9,36}... | collective-permute-start | bytes 786440 | tf_op jit(solution)/shard_map/ppermute | solution.py:264
Sparse Core Ops, SparseCore 0:
  94.4 21.7 all-gather.3

commit v3 on v2

--- a/solution.py
+++ b/solution.py
@@ -121,76 +121,378 @@
     )(dst, rel, rows, coeffs, basis_mats.reshape(bases, width, width))
 
 
-def terms_kernel(agg_ref, scaled_ref, out_ref):
-    group, part, n_ent = agg_ref.shape
-    terms = dot(agg_ref[...].reshape(group * part, n_ent), scaled_ref[...])
-    out_ref[...] = terms.astype(BF).reshape(out_ref.shape)
-
-
-def basis_terms(agg, scaled):
-    bases, part, n_ent = agg.shape
-    width = scaled.shape[1]
-    group = 8
-    return pl.pallas_call(
-        terms_kernel,
-        out_shape=jax.ShapeDtypeStruct((bases, part, width), BF),
-        grid=(bases // group,),
-        in_specs=[
-            pl.BlockSpec((group, part, n_ent), lambda i: (i, 0, 0)),
-            pl.BlockSpec((n_ent, width), lambda i: (0, 0)),
-        ],
-        out_specs=pl.BlockSpec((group, part, width), lambda i: (i, 0, 0)),
-        compiler_params=pltpu.CompilerParams(vmem_limit_bytes=32 * MIB),
-    )(agg, scaled)
-
-
-def backward_kernel(
-    group, scaled_ref, dst_ref, coef_t_ref, basis_hbm, out_ref, basis, pick, acc, sem
+def remote(src, dst, send_sem, recv_sem, z, e):
+    return pltpu.make_async_remote_copy(
+        src_ref=src,
+        dst_ref=dst,
+        send_sem=send_sem,
+        recv_sem=recv_sem,
+        device_id=(z, e),
+        device_id_type=pl.DeviceIdType.MESH,
+    )
+
+
+def finish_kernel(
+    n_z,
+    n_e,
+    sums_ref,
+    inv_ref,
+    feat_ref,
+    w_ref,
+    cot_ref,
+    src_ref,
+    dst_ref,
+    coef_t_ref,
+    agg_hbm,
+    basis_hbm,
+    act_ref,
+    gf_ref,
+    gb_ref,
+    sums_in,
+    pre_in,
+    scaled,
+    scaled_sib,
+    agg_own,
+    agg_sib,
+    basis,
+    pick,
+    pick_src,
+    acc,
+    term_out,
+    term_in,
+    row_out,
+    row_in,
+    load_sem,
+    sums_send,
+    sums_recv,
+    act_send,
+    act_recv,
+    pre_send,
+    pre_recv,
+    agg_send,
+    agg_recv,
+    sib_send,
+    sib_recv,
+    term_send,
+    term_recv,
+    row_send,
+    row_recv,
+    gf_send,
+    gf_recv,
 ):
     q = lax.axis_index("rel")
+    e = lax.axis_index("ent")
+    core = lax.rem(e, 2)
+    chip = lax.div(e, 2)
+    sib = e + 1 - 2 * core
     bases, part, width = basis.shape
-    load = pltpu.make_async_copy(
-        basis_hbm.at[:, pl.ds(pl.multiple_of(q * part, part), part), :], basis, sem
-    )
-    load.start()
+    half = bases // 2
+    n_chip = n_e // 2
+    per_z = bases // n_z
+    lanes = pl.ds(pl.multiple_of(q * part, part), part)
+
+    def owner(b):
+        return lax.div(b, per_z), lax.rem(b, per_z) * n_z + q
+
+    my_b = q * per_z + lax.div(e, n_z)
+    from_z = lax.rem(e, n_z)
+    from_core = lax.div(my_b, half)
+    self_owned = jnp.logical_and(from_z == q, from_core == core)
+
+    barrier = pltpu.get_barrier_semaphore()
+
+    def greet(z, peer):
+        pl.semaphore_signal(
+            barrier, inc=1, device_id=(z, peer), device_id_type=pl.DeviceIdType.MESH
+        )
+
+    for d in range(1, n_z):
+        greet(lax.rem(q + d, n_z), e)
+
+    def greet_plane(d, _):
+        greet(q, lax.rem(e + d, n_e))
+        return 0
+
+    lax.fori_loop(1, n_e, greet_plane, 0)
+
+    def greet_source(i, _):
+        source = i * 2 + from_core
+
+        @pl.when(jnp.logical_not(jnp.logical_and(from_z == q, source == e)))
+        def _():
+            greet(from_z, source)
+
+        return 0
+
+    lax.fori_loop(0, n_chip, greet_source, 0)
+
+    load_basis = pltpu.make_async_copy(basis_hbm.at[:, lanes, :], basis, load_sem.at[0])
+    load_basis.start()
+    load_agg = pltpu.make_async_copy(
+        agg_hbm.at[pl.ds(core * half, half)], agg_own, load_sem.at[1]
+    )
+    load_agg.start()
+    w_part = w_ref[:, lanes]
+    pre = dot(feat_ref[...], w_part)
+    pl.semaphore_wait(barrier, n_z - 1 + n_e - 1 + half - self_owned.astype(I32))
+
+    def sums_copy(d):
+        z = lax.rem(q + d, n_z)
+        return remote(
+            sums_ref.at[z], sums_in.at[q], sums_send.at[d], sums_recv.at[q], z, e
+        )
+
+    def sums_wait(d):
+        z = lax.rem(q + d, n_z)
+        remote(
+            sums_ref.at[z], sums_in.at[z], sums_send.at[d], sums_recv.at[z], z, e
+        ).wait_recv()
+
+    for d in range(1, n_z):
+        sums_copy(d).start()
+    agg_copy = remote(
+        agg_hbm.at[pl.ds((1 - core) * half, half)],
+        agg_sib,
+        agg_send,
+        agg_recv,
+        q,
+        sib,
+    )
+    agg_copy.start()
     pick[...] = one_hot(pick.shape[0], dst_ref[...])
+    pick_src[...] = one_hot(pick.shape[0], src_ref[...])
+    total = sums_ref[q].astype(F32)
+    for d in range(1, n_z):
+        sums_wait(d)
+        total += sums_in[lax.rem(q + d, n_z)].astype(F32)
+    inverse = inv_ref[...]
+    pre = pre + total * inverse
+    sig = jax.nn.sigmoid(pre)
+    slope = sig * (1.0 + pre * (1.0 - sig))
+    pre_in[q] = (cot_ref[:, lanes].astype(F32) * slope).astype(BF)
+
+    def pre_copy(d, z_in):
+        z = lax.rem(q + d, n_z)
+        return remote(pre_in.at[q], pre_in.at[z_in], pre_send.at[d], pre_recv.at[z_in], z, e)
+
+    def act_copy(d, z_in):
+        z = lax.rem(q + d, n_z)
+        at = pl.ds(pl.multiple_of(z_in * part, part), part)
+        return remote(
+            act_ref.at[:, lanes], act_ref.at[:, at], act_send.at[d], act_recv.at[z_in], z, e
+        )
+
+    for d in range(1, n_z):
+        pre_copy(d, q).start()
+    act_ref[:, lanes] = (pre * sig).astype(BF)
+    for d in range(1, n_z):
+        act_copy(d, q).start()
+    for d in range(1, n_z):
+        pre_copy(d, lax.rem(q + d, n_z)).wait_recv()
+    for z in range(n_z):
+        scaled[:, z * part : (z + 1) * part] = (pre_in[z].astype(F32) * inverse).astype(BF)
+    sib_copy = remote(scaled, scaled_sib, sib_send, sib_recv, q, sib)
+    sib_copy.start()
+    w_rows = w_ref[lanes, :]
+    grad = dot(pre_in[0], w_rows[:, :part], ((1,), (1,)))
+    for z in range(1, n_z):
+        grad += dot(pre_in[z], w_rows[:, z * part : (z + 1) * part], ((1,), (1,)))
+    load_agg.wait()
+    agg_copy.wait_recv()
+    sib_copy.wait_recv()
+
+    group = 4
+    groups = half // group
+    n_ent = agg_own.shape[2]
+
+    def term_copy(i):
+        z, peer = owner(core * half + i)
+        return remote(
+            term_out.at[i], term_in.at[chip], term_send.at[i], term_recv.at[chip], z, peer
+        )
+
+    def term_step(t, _):
+        first = lax.rem(t + chip, groups) * group
+        own = agg_own[pl.ds(first, group)].reshape(group * part, n_ent)
+        other = agg_sib[pl.ds(first, group)].reshape(group * part, n_ent)
+        terms = dot(own, scaled[...]) + dot(other, scaled_sib[...])
+        term_out[pl.ds(first, group)] = terms.astype(BF).reshape(group, part, width)
+        for g in range(group):
+            i = first + g
+            z, peer = owner(core * half + i)
+            mine = jnp.logical_and(z == q, peer == e)
+
+            @pl.when(mine)
+            def _():
+                term_in[chip] = term_out[i]
+
+            @pl.when(jnp.logical_not(mine))
+            def _():
+                term_copy(i).start()
+
+        return 0
+
+    lax.fori_loop(0, groups, term_step, 0)
     acc[...] = jnp.zeros_like(acc)
-    load.wait()
+    load_basis.wait()
 
     def step(i, _):
         weights = basis[pl.ds(i * group, group)].reshape(group * part, width)
-        back = dot(weights, scaled_ref[...], ((1,), (1,))).astype(BF)
+        back = dot(weights, scaled[...], ((1,), (1,))).astype(BF)
         spread = dot(back, pick[...])
-        total = acc[...]
+        rows = acc[...]
         for g in range(group):
-            total += (
-                spread[g * part : (g + 1) * part] * coef_t_ref[pl.ds(i * group + g, 1), :]
-            )
-        acc[...] = total
+            rows += spread[g * part : (g + 1) * part] * coef_t_ref[pl.ds(i * group + g, 1), :]
+        acc[...] = rows
         return 0
 
     lax.fori_loop(0, bases // group, step, 0)
-    out_ref[...] = acc[...].T.astype(BF)
-
-
-def backward(scaled, dst, coef_t, basis_mats):
+    row_out[...] = acc[...].T.astype(BF).reshape(row_out.shape)
+    row_in[e] = row_out[e]
+
+    def row_copy(peer, slot):
+        return remote(
+            row_out.at[peer], row_in.at[slot], row_send.at[peer], row_recv.at[slot], q, peer
+        )
+
+    def row_start(d, _):
+        row_copy(lax.rem(e + d, n_e), e).start()
+        return 0
+
+    def row_wait(d, _):
+        peer = lax.rem(e + d, n_e)
+        row_copy(peer, peer).wait_recv()
+        return 0
+
+    lax.fori_loop(1, n_e, row_start, 0)
+    lax.fori_loop(1, n_e, row_wait, 0)
+    grad += dot(pick_src[...], row_in[...].reshape(pick_src.shape[1], part))
+    gf_ref[:, lanes] = grad.astype(BF)
+
+    def gf_copy(d, z_in):
+        z = lax.rem(q + d, n_z)
+        at = pl.ds(pl.multiple_of(z_in * part, part), part)
+        return remote(
+            gf_ref.at[:, lanes], gf_ref.at[:, at], gf_send.at[d], gf_recv.at[z_in], z, e
+        )
+
+    for d in range(1, n_z):
+        gf_copy(d, q).start()
+
+    def term_wait(i, _):
+        source = i * 2 + from_core
+
+        @pl.when(jnp.logical_not(jnp.logical_and(from_z == q, source == e)))
+        def _():
+            remote(
+                term_out.at[0], term_in.at[i], term_send.at[0], term_recv.at[i], from_z, source
+            ).wait_recv()
+
+        return 0
+
+    lax.fori_loop(0, n_chip, term_wait, 0)
+    block = term_in[0].astype(F32)
+    for i in range(1, n_chip):
+        block += term_in[i].astype(F32)
+    gb_ref[...] = block
+
+    for d in range(1, n_z):
+        z = lax.rem(q + d, n_z)
+        act_copy(d, z).wait_recv()
+        gf_copy(d, z).wait_recv()
+        sums_copy(d).wait_send()
+        pre_copy(d, q).wait_send()
+        act_copy(d, q).wait_send()
+        gf_copy(d, q).wait_send()
+    agg_copy.wait_send()
+    sib_copy.wait_send()
+
+    def term_sent(i, _):
+        z, peer = owner(core * half + i)
+
+        @pl.when(jnp.logical_not(jnp.logical_and(z == q, peer == e)))
+        def _():
+            term_copy(i).wait_send()
+
+        return 0
+
+    lax.fori_loop(0, half, term_sent, 0)
+
+    def row_sent(d, _):
+        row_copy(lax.rem(e + d, n_e), e).wait_send()
+        return 0
+
+    lax.fori_loop(1, n_e, row_sent, 0)
+
+
+def finish(sums, inverse, features, w_self, cotangent, src, dst, coef_t, agg, basis_mats):
+    n_z = lax.axis_size("rel")
+    n_e = lax.axis_size("ent")
+    n_ent, width = features.shape
     bases, all_slots = coef_t.shape
-    n_ent, width = scaled.shape
-    part = 128
+    part = width // n_z
+    half = bases // 2
+    block = all_slots // n_e
     vm = pl.BlockSpec(memory_space=pltpu.VMEM)
+    hbm = pl.BlockSpec(memory_space=pl.ANY)
+    dma = pltpu.SemaphoreType.DMA
     return pl.pallas_call(
-        functools.partial(backward_kernel, 4),
-        out_shape=jax.ShapeDtypeStruct((all_slots, part), BF),
-        in_specs=[vm, vm, vm, pl.BlockSpec(memory_space=pl.ANY)],
-        out_specs=vm,
+        functools.partial(finish_kernel, n_z, n_e),
+        out_shape=(
+            jax.ShapeDtypeStruct((n_ent, width), BF),
+            jax.ShapeDtypeStruct((n_ent, width), BF),
+            jax.ShapeDtypeStruct((part, width), F32),
+        ),
+        in_specs=[vm] * 8 + [hbm, hbm],
+        out_specs=(vm, vm, vm),
         scratch_shapes=[
+            pltpu.VMEM((n_z, n_ent, part), BF),
+            pltpu.VMEM((n_z, n_ent, part), BF),
+            pltpu.VMEM((n_ent, width), BF),
+            pltpu.VMEM((n_ent, width), BF),
+            pltpu.VMEM((half, part, n_ent), BF),
+            pltpu.VMEM((half, part, n_ent), BF),
             pltpu.VMEM((bases, part, width), BF),
             pltpu.VMEM((n_ent, all_slots), BF),
+            pltpu.VMEM((n_ent, all_slots), BF),
             pltpu.VMEM((part, all_slots), F32),
-            pltpu.SemaphoreType.DMA,
+            pltpu.VMEM((half, part, width), BF),
+            pltpu.VMEM((n_e // 2, part, width), BF),
+            pltpu.VMEM((n_e, block, part), BF),
+            pltpu.VMEM((n_e, block, part), BF),
+            dma((2,)),
+            dma((n_z,)),
+            dma((n_z,)),
+            dma((n_z,)),
+            dma((n_z,)),
+            dma((n_z,)),
+            dma((n_z,)),
+            dma,
+            dma,
+            dma,
+            dma,
+            dma((half,)),
+            dma((n_e // 2,)),
+            dma((n_e,)),
+            dma((n_e,)),
+            dma((n_z,)),
+            dma((n_z,)),
         ],
-        compiler_params=pltpu.CompilerParams(vmem_limit_bytes=56 * MIB),
-    )(scaled, dst, coef_t, basis_mats.reshape(bases, width, width))
+        compiler_params=pltpu.CompilerParams(
+            vmem_limit_bytes=56 * MIB, collective_id=0, has_side_effects=True
+        ),
+    )(
+        sums,
+        inverse,
+        features,
+        w_self,
+        cotangent,
+        src,
+        dst,
+        coef_t,
+        agg,
+        basis_mats.reshape(bases, width, width),
+    )
 
 
 def per_device(
@@ -239,38 +541,9 @@
     rows = swap(rows.reshape(ent_count, rel_count * cap, part), "ent").reshape(all_slots, part)
 
     partial, agg, inverse, coef_t = forward(dst, rel, rows, basis_coeffs, basis_mats, n_ent)
-    partial = swap(partial, "rel")
-    sums = jnp.sum(partial.astype(F32), axis=0)
-
-    w_part = lax.dynamic_slice_in_dim(w_self, q * part, part, 1)
-    cot = lax.dynamic_slice_in_dim(cotangent, q * part, part, 1).astype(F32)
-    pre = dot(features, w_part) + sums * inverse
-    sig = jax.nn.sigmoid(pre)
-    act = (pre * sig).astype(BF)
-    grad_pre = (cot * (sig * (1.0 + pre * (1.0 - sig)))).astype(BF)
-    both = lax.all_gather(jnp.stack([act, grad_pre]), "rel")
-    act = both[:, 0].transpose(1, 0, 2).reshape(n_ent, width)
-    grad_pre = both[:, 1].transpose(1, 0, 2).reshape(n_ent, width)
-    scaled = (grad_pre.astype(F32) * inverse[:, :1]).astype(BF)
-
-    terms = swap(basis_terms(agg, scaled), "ent")
-    block = jnp.sum(terms.astype(F32), axis=0)
-    per_rel = bases // rel_count
-    routes = [
-        (r * ent_count + b, (b // per_rel) * ent_count + (b % per_rel) * rel_count + r)
-        for r in range(rel_count)
-        for b in range(bases)
-    ]
-    grad_basis = lax.ppermute(block, ("rel", "ent"), routes)
-
-    grad_rows = backward(scaled, dst, coef_t, basis_mats)
-    grad_rows = swap(grad_rows.reshape(ent_count, rel_count * cap, part), "ent")
-    w_rows = lax.dynamic_slice_in_dim(w_self, q * part, part, 0)
-    grad_part = dot(grad_pre, w_rows, ((1,), (1,))) + dot(
-        pick_src, grad_rows.reshape(all_slots, part)
-    )
-    grad_features = lax.all_gather(grad_part.astype(BF), "rel", axis=1, tiled=True)
-    return act, grad_features, grad_basis
+    return finish(
+        partial, inverse, features, w_self, cotangent, src, dst, coef_t, agg, basis_mats
+    )
 
 
 def solution(mesh):

time: 228 us -> 189 us (0.83)
  Pallas kernels: 44.8 us -> 134 us
  waiting for transfers between devices: 61 us -> 6.55 us
  blocking collectives: 41.3 us -> 10.6 us
  starting transfers between devices: 39.9 us -> 16.2 us
  between operations: 14.3 us -> 0.74 us
  other arithmetic: 6.87 us -> 3.08 us
    pallas_call x2 -> x1, Pallas kernels: 19.8 us -> 109 us  [finish(): pl.pallas_call(functools.partial(finish_kernel, n_z, n_e), out_shape=(jax...]
    all_to_all x4 -> x2, waiting for transfers between devices: 39.2 us -> 6.55 us  [swap(): return lax.all_to_all(x, axis, split_axis=0, concat_axis=0, tiled=True)]
    all_gather x1 -> x0, waiting for transfers between devices: 21.8 us -> none  [per_device(): both = lax.all_gather(jnp.stack([act, grad_pre]), 'rel')]
    all_to_all x4 -> x2, starting transfers between devices: 34.1 us -> 16.2 us  [swap(): return lax.all_to_all(x, axis, split_axis=0, concat_axis=0, tiled=True)]
    all_gather x1 -> x0, blocking collectives: 17.5 us -> none  [per_device(): lax.all_gather(grad_part.astype(BF), 'rel', axis=1, tiled=True)]
    all_to_all x1 -> x0, blocking collectives: 13.1 us -> none  [swap(): return lax.all_to_all(x, axis, split_axis=0, concat_axis=0, tiled=True)]
    ppermute x1 -> x0, starting transfers between devices: 5.77 us -> none  [per_device(): grad_basis = lax.ppermute(block, ('rel', 'ent'), routes)]
    reduce_sum x2 -> x0, other arithmetic: 2.87 us -> none  [the longest x1 2.8 us: per_device(): block = jnp.sum(terms.astype(F32), axis=0)]
  transfers between devices with their start and end apart: 6 -> 2, of which waited for: 5 -> 2; matrix products, arithmetic and copies ran while one was open for 5% -> 4% of each run, Pallas kernels for 7% -> 0%
where the time goes in v3:
time: 189 us; the launch traced here: 187 us
  Pallas kernels  134 us (71%)
  starting transfers between devices  16.2 us (9%)
  local copies, waits for them, and re-layouts  12.6 us (7%)
  blocking collectives  10.6 us (6%)
  waiting for transfers between devices  6.55 us (3%)
  other arithmetic  3.08 us (2%)
  matrix products  2.98 us (2%)
    pallas_call x1, Pallas kernels, finish(): pl.pallas_call(functools.partial(finish_kernel, n_z, n_e), out_shape=(jax...  109 us
    pallas_call x1, Pallas kernels, forward(): pl.pallas_call(functools.partial(forward_kernel, 2), out_shape=(jax.Shape...  25 us
    all_to_all x2, starting transfers between devices, swap(): return lax.all_to_all(x, axis, split_axis=0, concat_axis=0, tiled=True)  16.2 us
    all_gather x1, blocking collectives, per_device(): meta = lax.all_gather(meta, 'rel')  10.6 us
    unnamed x10, local copies, waits for them, and re-layouts  8.22 us
    all_to_all x2, waiting for transfers between devices, swap(): return lax.all_to_all(x, axis, split_axis=0, concat_axis=0, tiled=True)  6.55 us
  transfers between devices with their start and end apart: 2, of which 2 were waited for; matrix products, arithmetic and copies ran while one was open for 4% of the time, Pallas kernels for 0%

profile of v3, /device:TPU:25, one launch (start us, length us, event | category | flops | bytes accessed | tf_op | source)
XLA Modules:
  0.0 187.1 jit_solution(2047862721982666731)
XLA Ops:
  0.6 0.0 copy-start.1
  0.7 1.0 select_reduce_fusion
  1.6 0.1 stack_reshape.3
  1.7 0.7 broadcast_subtract_fusion
  2.4 0.1 sub.28
  2.5 0.8 reshape.101
  3.2 0.7 subtract_select_fusion
  4.0 0.1 copy.25
  4.1 10.6 %all-gather = s32[12,32,16]{1,2,0:T(8,128)S(1)} all-gather(s32[3,32,16]{1,2,0:T(8,128)S(1)} %copy.25), channel_id=2, replica_groups=mesh['rel'=4,'ent'=32] {'rel'}, dimensions={0}, use_global_device_ids=true | all-gather | bytes 30720 | tf_op jit(solution)/shard_map/all_gather | solution.py:531
  14.7 0.1 copy.26
  14.8 0.8 reshape.118
  15.6 10.2 %all-to-all-start = ((s32[32,1,128]{2,1,0:T(1,128)}), s32[32,1,128]{2,1,0:T(1,128)S(1)}, u32[]{:S(2)}, u32[]{:S(2)}) async-start(s32[32,1,128]{2,1,0:T(1,128)} %reshape.118), calls=%async_computation | async-start | bytes 32768 | tf_op jit(solution)/shard_map/all_to_all | solution.py:21
  25.8 0.1 copy.27
  25.9 0.1 eq.32
  26.0 3.0 %fusion.1 = bf16[2048,128]{1,0:T(8,128)(2,1)} fusion(s32[2048]{0:T(1024)S(1)} %eq.32, bf16[512,512]{1,0:T(8,128)(2,1)} %feat_ref.1, s32[]{:T(128)S(6)} %select_n.20), kind=kOutput, calls=%fused_computation.2 | convolution fusion | flops 269746176 | bytes 663556 | tf_op jit(solution)/shard_map/dot_general | solution.py:17
  29.0 1.9 %all-to-all-done = s32[32,1,128]{2,1,0:T(1,128)S(1)} async-done(((s32[32,1,128]{2,1,0:T(1,128)}), s32[32,1,128]{2,1,0:T(1,128)S(1)}, u32[]{:S(2)}, u32[]{:S(2)}) %all-to-all-start) | async-done | bytes 16416 | tf_op jit(solution)/shard_map/all_to_all | solution.py:21
  30.9 6.1 %all-to-all-start.1 = ((bf16[32,64,128]{2,1,0:T(8,128)(2,1)}), bf16[32,64,128]{2,1,0:T(8,128)(2,1)S(1)}, u32[]{:S(2)}, u32[]{:S(2)}) async-start(bf16[32,64,128]{2,1,0:T(8,128)(2,1)} %bitcast.4), calls=%async_computation.1 | async-start | bytes 1048576 | tf_op jit(solution)/shard_map/all_to_all | solution.py:21
  37.0 0.7 reshape_squeeze.11.src_ref
  37.7 0.0 copy-done.1
  37.7 1.0 copy.28.coef_ref
  38.7 0.5 broadcast.56
  39.2 0.7 reduce.8
  39.9 0.2 reshape.119
  40.1 0.4 slice_reduce_fusion
  40.5 0.7 reshape_squeeze.10.rel_ref
  41.2 0.7 reshape_squeeze.9.dst_ref
  41.9 4.6 %all-to-all-done.1 = bf16[32,64,128]{2,1,0:T(8,128)(2,1)S(1)} async-done(((bf16[32,64,128]{2,1,0:T(8,128)(2,1)}), bf16[32,64,128]{2,1,0:T(8,128)(2,1)S(1)}, u32[]{:S(2)}, u32[]{:S(2)}) %all-to-all-start.1) | async-done | bytes 524320 | tf_op jit(solution)/shard_map/all_to_all | solution.py:21
  46.6 0.0 copy-start
  46.6 0.8 copy-done
  47.4 25.0 %shard_map.121 = (bf16[4,512,128]{2,1,0:T(8,128)(2,1)}, bf16[32,128,512]{2,1,0:T(8,128)(2,1)}, f32[512,128]{1,0:T(8,128)}, f32[32,2048]{1,0:T(8,128)}) custom-call(s32[1,2048]{1,0:T(1,128)} %reshape_squeeze.9.dst_ref, s32[1,2048]{1,0:T(1,128)} %reshape_squeeze.10.rel_ref, bf16[2048,128]{1,0:T(8,128)(2,1)} %bitcast.15, f32[1000,32]{1,0:T(8,128)} %copy.28.coef_ref, ...), custom_call_target="tpu_custom_call" | custom-call | tf_op jit(solution)/shard_map/pallas_call | solution.py:102
  72.3 109.4 %shard_map.122 = (bf16[512,512]{1,0:T(8,128)(2,1)}, bf16[512,512]{1,0:T(8,128)(2,1)}, f32[128,512]{1,0:T(8,128)}) custom-call(bf16[4,512,128]{2,1,0:T(8,128)(2,1)} %get-tuple-element.7.sums_ref, f32[512,128]{1,0:T(8,128)} %get-tuple-element.8.inv_ref, bf16[512,512]{1,0:T(8,128)(2,1)} %feat_ref.1, bf16[512,512]{1,0:T(8,128)(2,1)} %w_ref.1, ...), custom_call_target="tpu_custom_call" | custom-call | tf_op jit(solution)/shard_map/pallas_call | solution.py:439
  181.7 1.9 copy.33
  183.6 1.9 copy.34
  185.5 1.7 copy.35
  (4 shorter events, 0.0 us)
Async XLA Ops:
  0.6 37.1 %copy-start.1 = (f32[1000,32]{0,1:T(8,128)S(1)}, f32[1000,32]{0,1:T(8,128)}, u32[]{:S(2)}) copy-start(f32[1000,32]{0,1:T(8,128)} %param.13) | copy-start | bytes 384004
  15.6 15.3 %all-to-all-start = ((s32[32,1,128]{2,1,0:T(1,128)}), s32[32,1,128]{2,1,0:T(1,128)S(1)}, u32[]{:S(2)}, u32[]{:S(2)}) async-start(s32[32,1,128]{2,1,0:T(1,128)} %reshape.118), calls=%async_computation | async-start | bytes 32768 | tf_op jit(solution)/shard_map/all_to_all | solution.py:21
  30.9 15.7 %all-to-all-start.1 = ((bf16[32,64,128]{2,1,0:T(8,128)(2,1)}), bf16[32,64,128]{2,1,0:T(8,128)(2,1)S(1)}, u32[]{:S(2)}, u32[]{:S(2)}) async-start(bf16[32,64,128]{2,1,0:T(8,128)(2,1)} %bitcast.4), calls=%async_computation.1 | async-start | bytes 1048576 | tf_op jit(solution)/shard_map/all_to_all | solution.py:21
  46.6 0.8 copy-start

commit v4 on v3

--- a/solution.py
+++ b/solution.py
@@ -32,6 +32,33 @@
     mid = rest.astype(BF)
     lo = (rest - mid.astype(F32)).astype(BF)
     return hi, mid, lo
+
+
+def slot_order(bases):
+    half = bases // 2
+    return [
+        c * half + (x % 2) * 8 + y * 2 + x // 2
+        for c in range(2)
+        for x in range(4)
+        for y in range(half // 4)
+    ]
+
+
+def basis_loads(basis_hbm, basis, sems, q):
+    part = basis.shape[1]
+    lanes = pl.ds(pl.multiple_of(q * part, part), part)
+    loads = []
+    for c in range(2):
+        for x in range(4):
+            at = c * 4 + x
+            loads.append(
+                pltpu.make_async_copy(
+                    basis_hbm.at[c, x % 2, :, x // 2, lanes, :],
+                    basis.at[pl.ds(at * 4, 4)],
+                    sems.at[at],
+                )
+            )
+    return loads
 
 
 def forward_kernel(
@@ -56,23 +83,24 @@
     bases, part, width = basis.shape
     rels = coef_ref.shape[0]
     n_ent = pick.shape[0]
-    load = pltpu.make_async_copy(
-        basis_hbm.at[:, pl.ds(pl.multiple_of(q * part, part), part), :], basis, sem
-    )
-    load.start()
+    loads = basis_loads(basis_hbm, basis, sem, q)
+    for load in loads:
+        load.start()
     table[...] = jnp.zeros_like(table)
     table[:rels, :bases] = coef_ref[...]
     which = one_hot(table.shape[0], rel_ref[...])
     hi, mid, lo = split3(table[...])
     coef_t = dot(hi, which, ((0,), (0,))) + dot(mid, which, ((0,), (0,)))
     coef_t = coef_t + dot(lo, which, ((0,), (0,)))
-    coef_t_ref[...] = coef_t[:bases, :]
+    for p, b in enumerate(slot_order(bases)):
+        coef_t_ref[p : p + 1, :] = coef_t[b : b + 1, :]
     pick[...] = one_hot(n_ent, dst_ref[...])
     degree = dot(pick[...], jnp.ones((pick.shape[1], part), BF))
     inv_ref[...] = 1.0 / jnp.maximum(degree, 1.0)
     rows_t[...] = rows_ref[...].astype(F32).T
     acc[...] = jnp.zeros_like(acc)
-    load.wait()
+    for load in loads:
+        load.wait()
 
     def step(i, _):
         mixed = jnp.concatenate(
@@ -115,10 +143,10 @@
             pltpu.VMEM((n_ent, all_slots), BF),
             pltpu.VMEM((part, all_slots), F32),
             pltpu.VMEM((n_ent, width), F32),
-            pltpu.SemaphoreType.DMA,
+            pltpu.SemaphoreType.DMA((bases // 4,)),
         ],
         compiler_params=pltpu.CompilerParams(vmem_limit_bytes=56 * MIB),
-    )(dst, rel, rows, coeffs, basis_mats.reshape(bases, width, width))
+    )(dst, rel, rows, coeffs, basis_mats.reshape(2, 2, 4, 2, width, width))
 
 
 def remote(src, dst, send_sem, recv_sem, z, e):
@@ -158,10 +186,19 @@
     pick,
     pick_src,
     acc,
-    term_out,
-    term_in,
+    back,
+    term_x,
+    term_y,
+    x_in,
+    y_in,
+    half_x,
+    half_y,
+    xy_in,
+    yx_in,
+    done,
     row_out,
     row_in,
+    basis_sem,
     load_sem,
     sums_send,
     sums_recv,
@@ -173,8 +210,16 @@
     agg_recv,
     sib_send,
     sib_recv,
-    term_send,
-    term_recv,
+    x_send,
+    x_recv,
+    y_send,
+    y_recv,
+    xy_send,
+    xy_recv,
+    yx_send,
+    yx_recv,
+    move_send,
+    move_recv,
     row_send,
     row_recv,
     gf_send,
@@ -187,17 +232,19 @@
     sib = e + 1 - 2 * core
     bases, part, width = basis.shape
     half = bases // 2
-    n_chip = n_e // 2
-    per_z = bases // n_z
     lanes = pl.ds(pl.multiple_of(q * part, part), part)
-
-    def owner(b):
-        return lax.div(b, per_z), lax.rem(b, per_z) * n_z + q
-
-    my_b = q * per_z + lax.div(e, n_z)
-    from_z = lax.rem(e, n_z)
-    from_core = lax.div(my_b, half)
-    self_owned = jnp.logical_and(from_z == q, from_core == core)
+    x = lax.rem(chip, 4)
+    y = lax.div(chip, 4)
+
+    def at_chip(y_at, x_at):
+        return (y_at * 4 + x_at) * 2 + core
+
+    to_z = 2 * core + lax.rem(x, 2)
+    to_e = (y * 4 + lax.div(x, 2) * 2 + lax.div(q, 2)) * 2 + lax.rem(q, 2)
+    from_z = lax.rem(x, 2) * 2 + core
+    from_e = (y * 4 + lax.div(x, 2) * 2 + lax.rem(q, 2)) * 2 + lax.div(q, 2)
+    keeps = jnp.logical_and(to_z == q, to_e == e)
+    moves = jnp.logical_not(keeps)
 
     barrier = pltpu.get_barrier_semaphore()
 
@@ -215,26 +262,20 @@
 
     lax.fori_loop(1, n_e, greet_plane, 0)
 
-    def greet_source(i, _):
-        source = i * 2 + from_core
-
-        @pl.when(jnp.logical_not(jnp.logical_and(from_z == q, source == e)))
-        def _():
-            greet(from_z, source)
-
-        return 0
-
-    lax.fori_loop(0, n_chip, greet_source, 0)
-
-    load_basis = pltpu.make_async_copy(basis_hbm.at[:, lanes, :], basis, load_sem.at[0])
-    load_basis.start()
+    @pl.when(moves)
+    def _():
+        greet(from_z, from_e)
+
+    loads = basis_loads(basis_hbm, basis, basis_sem, q)
+    for load in loads:
+        load.start()
     load_agg = pltpu.make_async_copy(
-        agg_hbm.at[pl.ds(core * half, half)], agg_own, load_sem.at[1]
+        agg_hbm.at[pl.ds(core * half, half)], agg_own, load_sem
     )
     load_agg.start()
     w_part = w_ref[:, lanes]
     pre = dot(feat_ref[...], w_part)
-    pl.semaphore_wait(barrier, n_z - 1 + n_e - 1 + half - self_owned.astype(I32))
+    pl.semaphore_wait(barrier, n_z - 1 + n_e - 1 + moves.astype(I32))
 
     def sums_copy(d):
         z = lax.rem(q + d, n_z)
@@ -286,8 +327,6 @@
         pre_copy(d, q).start()
     act_ref[:, lanes] = (pre * sig).astype(BF)
     for d in range(1, n_z):
-        act_copy(d, q).start()
-    for d in range(1, n_z):
         pre_copy(d, lax.rem(q + d, n_z)).wait_recv()
     for z in range(n_z):
         scaled[:, z * part : (z + 1) * part] = (pre_in[z].astype(F32) * inverse).astype(BF)
@@ -302,61 +341,86 @@
     sib_copy.wait_recv()
 
     group = 4
-    groups = half // group
     n_ent = agg_own.shape[2]
-
-    def term_copy(i):
-        z, peer = owner(core * half + i)
-        return remote(
-            term_out.at[i], term_in.at[chip], term_send.at[i], term_recv.at[chip], z, peer
-        )
-
-    def term_step(t, _):
-        first = lax.rem(t + chip, groups) * group
-        own = agg_own[pl.ds(first, group)].reshape(group * part, n_ent)
-        other = agg_sib[pl.ds(first, group)].reshape(group * part, n_ent)
+    wide = width // 2
+
+    def x_first(d, slot):
+        peer = lax.rem(x + d, 4)
+        return remote(
+            term_x.at[peer], x_in.at[slot], x_send.at[d], x_recv.at[slot], q, at_chip(y, peer)
+        )
+
+    def y_first(d, slot):
+        peer = lax.rem(y + d, 4)
+        return remote(
+            term_y.at[peer], y_in.at[slot], y_send.at[d], y_recv.at[slot], q, at_chip(peer, x)
+        )
+
+    def x_then_y(d, slot):
+        peer = lax.rem(y + d, 4)
+        return remote(
+            half_x.at[peer], xy_in.at[slot], xy_send.at[d], xy_recv.at[slot], q, at_chip(peer, x)
+        )
+
+    def y_then_x(d, slot):
+        peer = lax.rem(x + d, 4)
+        return remote(
+            half_y.at[peer], yx_in.at[slot], yx_send.at[d], yx_recv.at[slot], q, at_chip(y, peer)
+        )
+
+    for d in (2, 1, 3, 0):
+        at = lax.rem(x + d, 4)
+        own = agg_own[pl.ds(at * group, group)].reshape(group * part, n_ent)
+        other = agg_sib[pl.ds(at * group, group)].reshape(group * part, n_ent)
         terms = dot(own, scaled[...]) + dot(other, scaled_sib[...])
-        term_out[pl.ds(first, group)] = terms.astype(BF).reshape(group, part, width)
+        terms = terms.astype(BF)
+        term_x[at] = terms[:, :wide].reshape(group, part, wide)
         for g in range(group):
-            i = first + g
-            z, peer = owner(core * half + i)
-            mine = jnp.logical_and(z == q, peer == e)
-
-            @pl.when(mine)
-            def _():
-                term_in[chip] = term_out[i]
-
-            @pl.when(jnp.logical_not(mine))
-            def _():
-                term_copy(i).start()
-
+            term_y[g, at] = terms[g * part : (g + 1) * part, wide:]
+        if d:
+            x_first(d, x).start()
+    for d in (2, 1, 3):
+        y_first(d, y).start()
+    for d in range(1, n_z):
+        act_copy(d, q).start()
+    for load in loads:
+        load.wait()
+    seg = acc.shape[1]
+
+    def back_step(i, _):
+        weights = basis[pl.ds(i * group, group)].reshape(group * part, width)
+        back[i] = dot(weights, scaled[...], ((1,), (1,))).astype(BF)
         return 0
 
-    lax.fori_loop(0, groups, term_step, 0)
-    acc[...] = jnp.zeros_like(acc)
-    load_basis.wait()
-
-    def step(i, _):
-        weights = basis[pl.ds(i * group, group)].reshape(group * part, width)
-        back = dot(weights, scaled[...], ((1,), (1,))).astype(BF)
-        spread = dot(back, pick[...])
-        rows = acc[...]
-        for g in range(group):
-            rows += spread[g * part : (g + 1) * part] * coef_t_ref[pl.ds(i * group + g, 1), :]
-        acc[...] = rows
-        return 0
-
-    lax.fori_loop(0, bases // group, step, 0)
-    row_out[...] = acc[...].T.astype(BF).reshape(row_out.shape)
-    row_in[e] = row_out[e]
+    lax.fori_loop(0, bases // group, back_step, 0)
+
+    def spread(first):
+        acc[...] = jnp.zeros_like(acc)
+
+        def step(i, _):
+            out = dot(back[i], pick[:, first : first + seg])
+            rows = acc[...]
+            for g in range(group):
+                coef = coef_t_ref[pl.ds(i * group + g, 1), first : first + seg]
+                rows += out[g * part : (g + 1) * part] * coef
+            acc[...] = rows
+            return 0
+
+        lax.fori_loop(0, bases // group, step, 0)
+        block = row_out.shape[1]
+        rows = acc[...].T.astype(BF).reshape(seg // block, block, part)
+        row_out[first // block : (first + seg) // block] = rows
 
     def row_copy(peer, slot):
         return remote(
             row_out.at[peer], row_in.at[slot], row_send.at[peer], row_recv.at[slot], q, peer
         )
 
-    def row_start(d, _):
-        row_copy(lax.rem(e + d, n_e), e).start()
+    def row_start(peer, _):
+        @pl.when(peer != e)
+        def _():
+            row_copy(peer, e).start()
+
         return 0
 
     def row_wait(d, _):
@@ -364,7 +428,26 @@
         row_copy(peer, peer).wait_recv()
         return 0
 
-    lax.fori_loop(1, n_e, row_start, 0)
+    per_seg = n_e * seg // pick.shape[1]
+    for n in range(n_e // per_seg):
+        spread(n * seg)
+        lax.fori_loop(n * per_seg, (n + 1) * per_seg, row_start, 0)
+    row_in[e] = row_out[e]
+
+    def add_up(own, arrived, recv, me):
+        total = own.astype(F32)
+        for d in (1, 3, 2):
+            slot = lax.rem(me + d, 4)
+            recv(d, slot).wait_recv()
+            total += arrived[slot].astype(F32)
+        return total
+
+    half_x[...] = add_up(term_x[x], x_in, x_first, x).astype(BF)
+    for d in (2, 1, 3):
+        x_then_y(d, y).start()
+    half_y[...] = add_up(term_y[y], y_in, y_first, y).astype(BF)
+    for d in (2, 1, 3):
+        y_then_x(d, x).start()
     lax.fori_loop(1, n_e, row_wait, 0)
     grad += dot(pick_src[...], row_in[...].reshape(pick_src.shape[1], part))
     gf_ref[:, lanes] = grad.astype(BF)
@@ -379,22 +462,19 @@
     for d in range(1, n_z):
         gf_copy(d, q).start()
 
-    def term_wait(i, _):
-        source = i * 2 + from_core
-
-        @pl.when(jnp.logical_not(jnp.logical_and(from_z == q, source == e)))
-        def _():
-            remote(
-                term_out.at[0], term_in.at[i], term_send.at[0], term_recv.at[i], from_z, source
-            ).wait_recv()
-
-        return 0
-
-    lax.fori_loop(0, n_chip, term_wait, 0)
-    block = term_in[0].astype(F32)
-    for i in range(1, n_chip):
-        block += term_in[i].astype(F32)
-    gb_ref[...] = block
+    done[:, :wide] = add_up(half_x[y], xy_in, x_then_y, y)
+    done[:, wide:] = add_up(half_y[x], yx_in, y_then_x, x)
+    move = remote(done, gb_ref, move_send, move_recv, to_z, to_e)
+
+    @pl.when(keeps)
+    def _():
+        gb_ref[...] = done[...]
+
+    @pl.when(moves)
+    def _():
+        move.start()
+        move.wait_send()
+        remote(done, gb_ref, move_send, move_recv, from_z, from_e).wait_recv()
 
     for d in range(1, n_z):
         z = lax.rem(q + d, n_z)
@@ -407,16 +487,11 @@
     agg_copy.wait_send()
     sib_copy.wait_send()
 
-    def term_sent(i, _):
-        z, peer = owner(core * half + i)
-
-        @pl.when(jnp.logical_not(jnp.logical_and(z == q, peer == e)))
-        def _():
-            term_copy(i).wait_send()
-
-        return 0
-
-    lax.fori_loop(0, half, term_sent, 0)
+    for d in (1, 2, 3):
+        x_first(d, x).wait_send()
+        y_first(d, y).wait_send()
+        x_then_y(d, y).wait_send()
+        y_then_x(d, x).wait_send()
 
     def row_sent(d, _):
         row_copy(lax.rem(e + d, n_e), e).wait_send()
@@ -455,12 +530,21 @@
             pltpu.VMEM((bases, part, width), BF),
             pltpu.VMEM((n_ent, all_slots), BF),
             pltpu.VMEM((n_ent, all_slots), BF),
-            pltpu.VMEM((part, all_slots), F32),
-            pltpu.VMEM((half, part, width), BF),
-            pltpu.VMEM((n_e // 2, part, width), BF),
+            pltpu.VMEM((part, all_slots // 2), F32),
+            pltpu.VMEM((bases // 4, 4 * part, n_ent), BF),
+            pltpu.VMEM((4, 4, part, width // 2), BF),
+            pltpu.VMEM((4, 4, part, width // 2), BF),
+            pltpu.VMEM((4, 4, part, width // 2), BF),
+            pltpu.VMEM((4, 4, part, width // 2), BF),
+            pltpu.VMEM((4, part, width // 2), BF),
+            pltpu.VMEM((4, part, width // 2), BF),
+            pltpu.VMEM((4, part, width // 2), BF),
+            pltpu.VMEM((4, part, width // 2), BF),
+            pltpu.VMEM((part, width), F32),
             pltpu.VMEM((n_e, block, part), BF),
             pltpu.VMEM((n_e, block, part), BF),
-            dma((2,)),
+            dma((bases // 4,)),
+            dma,
             dma((n_z,)),
             dma((n_z,)),
             dma((n_z,)),
@@ -471,8 +555,16 @@
             dma,
             dma,
             dma,
-            dma((half,)),
-            dma((n_e // 2,)),
+            dma((4,)),
+            dma((4,)),
+            dma((4,)),
+            dma((4,)),
+            dma((4,)),
+            dma((4,)),
+            dma((4,)),
+            dma((4,)),
+            dma,
+            dma,
             dma((n_e,)),
             dma((n_e,)),
             dma((n_z,)),
@@ -491,7 +583,7 @@
         dst,
         coef_t,
         agg,
-        basis_mats.reshape(bases, width, width),
+        basis_mats.reshape(2, 2, 4, 2, width, width),
     )
 
 

time: 189 us -> 149 us (0.79)
  Pallas kernels: 134 us -> 95.7 us
    pallas_call x1, Pallas kernels: 109 us -> 70.6 us  [finish(): pl.pallas_call(functools.partial(finish_kernel, n_z, n_e), out_shape=(jax...]
  transfers between devices with their start and end apart: 2 -> 2, of which waited for: 2 -> 2; matrix products, arithmetic and copies ran while one was open for 4% -> 5% of each run, Pallas kernels for 0% -> 0%
where the time goes in v4:
time: 149 us
  Pallas kernels  95.7 us (64%)
  starting transfers between devices  16.2 us (11%)
  local copies, waits for them, and re-layouts  12.6 us (8%)
  blocking collectives  10.6 us (7%)
  waiting for transfers between devices  6.56 us (4%)
  other arithmetic  3.08 us (2%)
  matrix products  2.98 us (2%)
    pallas_call x1, Pallas kernels, finish(): pl.pallas_call(functools.partial(finish_kernel, n_z, n_e), out_shape=(jax...  70.6 us
    pallas_call x1, Pallas kernels, forward(): pl.pallas_call(functools.partial(forward_kernel, 2), out_shape=(jax.Shape...  25.1 us
    all_to_all x2, starting transfers between devices, swap(): return lax.all_to_all(x, axis, split_axis=0, concat_axis=0, tiled=True)  16.2 us
    all_gather x1, blocking collectives, per_device(): meta = lax.all_gather(meta, 'rel')  10.6 us
    unnamed x10, local copies, waits for them, and re-layouts  8.22 us
    all_to_all x2, waiting for transfers between devices, swap(): return lax.all_to_all(x, axis, split_axis=0, concat_axis=0, tiled=True)  6.56 us
    dot_general x1, matrix products, dot(): return lax.dot_general(a, b, (dims, ((), ())), preferred_element_type=F32)  2.98 us
  transfers between devices with their start and end apart: 2, of which 2 were waited for; matrix products, arithmetic and copies ran while one was open for 5% of the time, Pallas kernels for 0%

profile of v4, /device:TPU:25, one launch (start us, length us, event | category | flops | bytes accessed | tf_op | source)
XLA Modules:
  0.0 148.5 jit_solution(14608679320686099753)
XLA Ops:
  0.6 0.0 copy-start.1
  0.7 1.0 select_reduce_fusion
  1.6 0.1 stack_reshape.3
  1.7 0.7 broadcast_subtract_fusion
  2.4 0.1 sub.28
  2.5 0.8 reshape.101
  3.2 0.7 subtract_select_fusion
  4.0 0.1 copy.25
  4.1 10.6 %all-gather = s32[12,32,16]{1,2,0:T(8,128)S(1)} all-gather(s32[3,32,16]{1,2,0:T(8,128)S(1)} %copy.25), channel_id=2, replica_groups=mesh['rel'=4,'ent'=32] {'rel'}, dimensions={0}, use_global_device_ids=true | all-gather | bytes 30720 | tf_op jit(solution)/shard_map/all_gather | solution.py:623
  14.7 0.1 copy.26
  14.8 0.8 reshape.118
  15.6 10.2 %all-to-all-start = ((s32[32,1,128]{2,1,0:T(1,128)}), s32[32,1,128]{2,1,0:T(1,128)S(1)}, u32[]{:S(2)}, u32[]{:S(2)}) async-start(s32[32,1,128]{2,1,0:T(1,128)} %reshape.118), calls=%async_computation | async-start | bytes 32768 | tf_op jit(solution)/shard_map/all_to_all | solution.py:21
  25.8 0.1 copy.27
  25.9 0.1 eq.32
  26.0 3.0 %fusion.1 = bf16[2048,128]{1,0:T(8,128)(2,1)} fusion(s32[2048]{0:T(1024)S(1)} %eq.32, bf16[512,512]{1,0:T(8,128)(2,1)} %feat_ref.1, s32[]{:T(128)S(6)} %select_n.20), kind=kOutput, calls=%fused_computation.2 | convolution fusion | flops 269746176 | bytes 663556 | tf_op jit(solution)/shard_map/dot_general | solution.py:17
  29.0 1.9 %all-to-all-done = s32[32,1,128]{2,1,0:T(1,128)S(1)} async-done(((s32[32,1,128]{2,1,0:T(1,128)}), s32[32,1,128]{2,1,0:T(1,128)S(1)}, u32[]{:S(2)}, u32[]{:S(2)}) %all-to-all-start) | async-done | bytes 16416 | tf_op jit(solution)/shard_map/all_to_all | solution.py:21
  30.9 6.1 %all-to-all-start.1 = ((bf16[32,64,128]{2,1,0:T(8,128)(2,1)}), bf16[32,64,128]{2,1,0:T(8,128)(2,1)S(1)}, u32[]{:S(2)}, u32[]{:S(2)}) async-start(bf16[32,64,128]{2,1,0:T(8,128)(2,1)} %bitcast.4), calls=%async_computation.1 | async-start | bytes 1048576 | tf_op jit(solution)/shard_map/all_to_all | solution.py:21
  37.0 0.7 reshape_squeeze.11.src_ref
  37.7 0.0 copy-done.1
  37.7 1.0 copy.28.coef_ref
  38.7 0.5 broadcast.56
  39.2 0.7 reduce.8
  39.9 0.2 reshape.119
  40.1 0.4 slice_reduce_fusion
  40.5 0.7 reshape_squeeze.10.rel_ref
  41.2 0.7 reshape_squeeze.9.dst_ref
  41.9 4.7 %all-to-all-done.1 = bf16[32,64,128]{2,1,0:T(8,128)(2,1)S(1)} async-done(((bf16[32,64,128]{2,1,0:T(8,128)(2,1)}), bf16[32,64,128]{2,1,0:T(8,128)(2,1)S(1)}, u32[]{:S(2)}, u32[]{:S(2)}) %all-to-all-start.1) | async-done | bytes 524320 | tf_op jit(solution)/shard_map/all_to_all | solution.py:21
  46.6 0.0 copy-start
  46.6 0.8 copy-done
  47.4 25.1 %shard_map.121 = (bf16[4,512,128]{2,1,0:T(8,128)(2,1)}, bf16[32,128,512]{2,1,0:T(8,128)(2,1)}, f32[512,128]{1,0:T(8,128)}, f32[32,2048]{1,0:T(8,128)}) custom-call(s32[1,2048]{1,0:T(1,128)} %reshape_squeeze.9.dst_ref, s32[1,2048]{1,0:T(1,128)} %reshape_squeeze.10.rel_ref, bf16[2048,128]{1,0:T(8,128)(2,1)} %bitcast.15, f32[1000,32]{1,0:T(8,128)} %copy.28.coef_ref, ...), custom_call_target="tpu_custom_call" | custom-call | tf_op jit(solution)/shard_map/pallas_call | solution.py:130
  72.5 70.6 %shard_map.122 = (bf16[512,512]{1,0:T(8,128)(2,1)}, bf16[512,512]{1,0:T(8,128)(2,1)}, f32[128,512]{1,0:T(8,128)}) custom-call(bf16[4,512,128]{2,1,0:T(8,128)(2,1)} %get-tuple-element.7.sums_ref, f32[512,128]{1,0:T(8,128)} %get-tuple-element.8.inv_ref, bf16[512,512]{1,0:T(8,128)(2,1)} %feat_ref.1, bf16[512,512]{1,0:T(8,128)(2,1)} %w_ref.1, ...), custom_call_target="tpu_custom_call" | custom-call | tf_op jit(solution)/shard_map/pallas_call | solution.py:514
  143.1 1.9 %copy.33 = bf16[512,512]{1,0:T(8,128)(2,1)} copy(bf16[512,512]{1,0:T(8,128)(2,1)} %get-tuple-element.16) | data formatting | bytes 1048576
  145.0 1.9 %copy.34 = bf16[512,512]{1,0:T(8,128)(2,1)} copy(bf16[512,512]{1,0:T(8,128)(2,1)} %get-tuple-element.17) | data formatting | bytes 1048576
  146.8 1.7 %copy.35 = f32[128,512]{1,0:T(8,128)} copy(f32[128,512]{1,0:T(8,128)} %get-tuple-element.18) | data formatting | bytes 524288
  (4 shorter events, 0.0 us)
Async XLA Ops:
  0.6 37.1 %copy-start.1 = (f32[1000,32]{0,1:T(8,128)S(1)}, f32[1000,32]{0,1:T(8,128)}, u32[]{:S(2)}) copy-start(f32[1000,32]{0,1:T(8,128)} %param.13) | copy-start | bytes 384004
  15.6 15.3 %all-to-all-start = ((s32[32,1,128]{2,1,0:T(1,128)}), s32[32,1,128]{2,1,0:T(1,128)S(1)}, u32[]{:S(2)}, u32[]{:S(2)}) async-start(s32[32,1,128]{2,1,0:T(1,128)} %reshape.118), calls=%async_computation | async-start | bytes 32768 | tf_op jit(solution)/shard_map/all_to_all | solution.py:21
  30.9 15.7 %all-to-all-start.1 = ((bf16[32,64,128]{2,1,0:T(8,128)(2,1)}), bf16[32,64,128]{2,1,0:T(8,128)(2,1)S(1)}, u32[]{:S(2)}, u32[]{:S(2)}) async-start(bf16[32,64,128]{2,1,0:T(8,128)(2,1)} %bitcast.4), calls=%async_computation.1 | async-start | bytes 1048576 | tf_op jit(solution)/shard_map/all_to_all | solution.py:21
  46.6 0.8 copy-start

commit v5 on v4

--- a/solution.py
+++ b/solution.py
@@ -15,10 +15,6 @@
 
 def dot(a, b, dims=((1,), (0,))):
     return lax.dot_general(a, b, (dims, ((), ())), preferred_element_type=F32)
-
-
-def swap(x, axis):
-    return lax.all_to_all(x, axis, split_axis=0, concat_axis=0, tiled=True)
 
 
 def one_hot(count, row):
@@ -61,94 +57,6 @@
     return loads
 
 
-def forward_kernel(
-    group,
-    dst_ref,
-    rel_ref,
-    rows_ref,
-    coef_ref,
-    basis_hbm,
-    part_ref,
-    agg_ref,
-    inv_ref,
-    coef_t_ref,
-    basis,
-    table,
-    pick,
-    rows_t,
-    acc,
-    sem,
-):
-    q = lax.axis_index("rel")
-    bases, part, width = basis.shape
-    rels = coef_ref.shape[0]
-    n_ent = pick.shape[0]
-    loads = basis_loads(basis_hbm, basis, sem, q)
-    for load in loads:
-        load.start()
-    table[...] = jnp.zeros_like(table)
-    table[:rels, :bases] = coef_ref[...]
-    which = one_hot(table.shape[0], rel_ref[...])
-    hi, mid, lo = split3(table[...])
-    coef_t = dot(hi, which, ((0,), (0,))) + dot(mid, which, ((0,), (0,)))
-    coef_t = coef_t + dot(lo, which, ((0,), (0,)))
-    for p, b in enumerate(slot_order(bases)):
-        coef_t_ref[p : p + 1, :] = coef_t[b : b + 1, :]
-    pick[...] = one_hot(n_ent, dst_ref[...])
-    degree = dot(pick[...], jnp.ones((pick.shape[1], part), BF))
-    inv_ref[...] = 1.0 / jnp.maximum(degree, 1.0)
-    rows_t[...] = rows_ref[...].astype(F32).T
-    acc[...] = jnp.zeros_like(acc)
-    for load in loads:
-        load.wait()
-
-    def step(i, _):
-        mixed = jnp.concatenate(
-            [
-                (rows_t[...] * coef_t_ref[pl.ds(i * group + g, 1), :]).astype(BF)
-                for g in range(group)
-            ],
-            axis=0,
-        )
-        agg = dot(pick[...], mixed, ((1,), (1,)))
-        agg_b = agg.astype(BF)
-        weights = basis[pl.ds(i * group, group)].reshape(group * part, width)
-        acc[...] += dot(agg_b, weights)
-        agg_ref[pl.ds(i * group, group)] = agg.T.astype(BF).reshape(group, part, n_ent)
-        return 0
-
-    lax.fori_loop(0, bases // group, step, 0)
-    for r in range(width // part):
-        part_ref[r] = acc[:, r * part : (r + 1) * part].astype(BF)
-
-
-def forward(dst, rel, rows, coeffs, basis_mats, n_ent):
-    all_slots, part = rows.shape
-    rels, bases = coeffs.shape
-    width = basis_mats.shape[1]
-    vm = pl.BlockSpec(memory_space=pltpu.VMEM)
-    return pl.pallas_call(
-        functools.partial(forward_kernel, 2),
-        out_shape=(
-            jax.ShapeDtypeStruct((width // part, n_ent, part), BF),
-            jax.ShapeDtypeStruct((bases, part, n_ent), BF),
-            jax.ShapeDtypeStruct((n_ent, part), F32),
-            jax.ShapeDtypeStruct((bases, all_slots), F32),
-        ),
-        in_specs=[vm, vm, vm, vm, pl.BlockSpec(memory_space=pl.ANY)],
-        out_specs=(vm, vm, vm, vm),
-        scratch_shapes=[
-            pltpu.VMEM((bases, part, width), BF),
-            pltpu.VMEM((1024, 128), F32),
-            pltpu.VMEM((n_ent, all_slots), BF),
-            pltpu.VMEM((part, all_slots), F32),
-            pltpu.VMEM((n_ent, width), F32),
-            pltpu.SemaphoreType.DMA((bases // 4,)),
-        ],
-        compiler_params=pltpu.CompilerParams(vmem_limit_bytes=56 * MIB),
-    )(dst, rel, rows, coeffs, basis_mats.reshape(2, 2, 4, 2, width, width))
-
-
 def remote(src, dst, send_sem, recv_sem, z, e):
     return pltpu.make_async_remote_copy(
         src_ref=src,
@@ -160,27 +68,37 @@
     )
 
 
-def finish_kernel(
+def step_kernel(
     n_z,
     n_e,
-    sums_ref,
-    inv_ref,
+    meta_ref,
     feat_ref,
     w_ref,
     cot_ref,
-    src_ref,
-    dst_ref,
-    coef_t_ref,
-    agg_hbm,
+    coef_ref,
     basis_hbm,
     act_ref,
     gf_ref,
     gb_ref,
+    meta_z,
+    meta_all,
+    tags,
+    line,
+    line_rel,
+    table,
+    feed_out,
+    feed_in,
+    rows_t,
+    coef_t_ref,
+    inv_ref,
+    pre_self,
+    sums_acc,
+    sums_ref,
+    agg,
     sums_in,
     pre_in,
     scaled,
     scaled_sib,
-    agg_own,
     agg_sib,
     basis,
     pick,
@@ -199,7 +117,6 @@
     row_out,
     row_in,
     basis_sem,
-    load_sem,
     sums_send,
     sums_recv,
     act_send,
@@ -224,6 +141,12 @@
     row_recv,
     gf_send,
     gf_recv,
+    meta_send,
+    meta_recv,
+    tag_send,
+    tag_recv,
+    feed_send,
+    feed_recv,
 ):
     q = lax.axis_index("rel")
     e = lax.axis_index("ent")
@@ -269,13 +192,122 @@
     loads = basis_loads(basis_hbm, basis, basis_sem, q)
     for load in loads:
         load.start()
-    load_agg = pltpu.make_async_copy(
-        agg_hbm.at[pl.ds(core * half, half)], agg_own, load_sem
+    table[...] = jnp.zeros_like(table)
+    table[: coef_ref.shape[0], :bases] = coef_ref[...]
+    pre_self[...] = dot(feat_ref[...], w_ref[:, lanes])
+    pl.semaphore_wait(barrier, n_z - 1 + n_e - 1 + moves.astype(I32))
+
+    def meta_copy(d, slot):
+        z = lax.rem(q + d, n_z)
+        return remote(meta_ref, meta_z.at[slot], meta_send.at[d], meta_recv.at[slot], z, e)
+
+    def tag_copy(peer, slot):
+        return remote(
+            meta_all.at[lax.div(peer, 2)],
+            tags.at[slot],
+            tag_send.at[peer],
+            tag_recv.at[slot],
+            q,
+            peer,
+        )
+
+    def feed_copy(peer, slot):
+        return remote(
+            feed_out.at[peer], feed_in.at[slot], feed_send.at[peer], feed_recv.at[slot], q, peer
+        )
+
+    def start_all(copy):
+        def go(d, _):
+            copy(lax.rem(e + d, n_e), e).start()
+            return 0
+
+        lax.fori_loop(1, n_e, go, 0)
+
+    def wait_all(copy):
+        def go(d, _):
+            peer = lax.rem(e + d, n_e)
+            copy(peer, peer).wait_recv()
+            return 0
+
+        lax.fori_loop(1, n_e, go, 0)
+
+    def sent_all(copy):
+        def go(d, _):
+            copy(lax.rem(e + d, n_e), e).wait_send()
+            return 0
+
+        lax.fori_loop(1, n_e, go, 0)
+
+    for d in range(1, n_z):
+        meta_copy(d, q).start()
+    feat_t = feat_ref[:, lanes].T
+    meta = meta_ref[...]
+    for d in range(1, n_z):
+        slot = lax.rem(q + d, n_z)
+        meta_copy(d, slot).wait_recv()
+        meta += meta_z[slot]
+    meta_all[...] = meta
+    start_all(tag_copy)
+    tags[e] = meta_all[lax.div(e, 2)]
+    n_ent = pick.shape[0]
+    pairs = n_e // 2
+    wide_lanes = meta_ref.shape[3]
+    for t in range(pairs):
+        line[:, t * wide_lanes : (t + 1) * wide_lanes] = meta_all[t, 0]
+    pick_src[...] = one_hot(n_ent, line[...])
+    feed = dot(feat_t, pick_src[...])
+    feed_out[...] = feed.T.astype(BF).reshape(feed_out.shape)
+    start_all(feed_copy)
+    feed_in[e] = feed_out[e]
+    wait_all(tag_copy)
+    left = lax.broadcasted_iota(I32, (1, wide_lanes), 1) < wide_lanes // 2
+    for f, out in ((1, line), (2, line_rel)):
+        for t in range(pairs):
+            even = tags[2 * t, f]
+            odd = tags[2 * t + 1, f]
+            even = jnp.where(core == 0, even, pltpu.roll(even, wide_lanes // 2, 1))
+            odd = jnp.where(core == 0, pltpu.roll(odd, wide_lanes // 2, 1), odd)
+            out[:, t * wide_lanes : (t + 1) * wide_lanes] = jnp.where(left, even, odd)
+    which = one_hot(table.shape[0], line_rel[...])
+    hi, mid, lo = split3(table[...])
+    coef_t = dot(hi, which, ((0,), (0,))) + dot(mid, which, ((0,), (0,)))
+    coef_t = coef_t + dot(lo, which, ((0,), (0,)))
+    for p, b in enumerate(slot_order(bases)):
+        coef_t_ref[p : p + 1, :] = coef_t[b : b + 1, :]
+    pick[...] = one_hot(n_ent, line[...])
+    degree = dot(pick[...], jnp.ones((pick.shape[1], part), BF))
+    inv_ref[...] = 1.0 / jnp.maximum(degree, 1.0)
+    sums_acc[...] = jnp.zeros_like(sums_acc)
+    wait_all(feed_copy)
+    rows_t[...] = feed_in[...].reshape(pick.shape[1], part).astype(F32).T
+    for load in loads:
+        load.wait()
+    pair = 2
+
+    def forward_step(i, _):
+        at = i * pair
+        mixed = jnp.concatenate(
+            [
+                (rows_t[...] * coef_t_ref[pl.ds(at + g, 1), :]).astype(BF)
+                for g in range(pair)
+            ],
+            axis=0,
+        )
+        out = dot(pick[...], mixed, ((1,), (1,)))
+        weights = basis[pl.ds(at, pair)].reshape(pair * part, width)
+        sums_acc[...] += dot(out.astype(BF), weights)
+        agg[pl.ds(at, pair)] = out.T.astype(BF).reshape(pair, part, n_ent)
+        return 0
+
+    agg_copy = remote(
+        agg.at[pl.ds((1 - core) * half, half)], agg_sib, agg_send, agg_recv, q, sib
     )
-    load_agg.start()
-    w_part = w_ref[:, lanes]
-    pre = dot(feat_ref[...], w_part)
-    pl.semaphore_wait(barrier, n_z - 1 + n_e - 1 + moves.astype(I32))
+    steps = half // pair
+    lax.fori_loop((1 - core) * steps, (2 - core) * steps, forward_step, 0)
+    agg_copy.start()
+    lax.fori_loop(core * steps, (1 + core) * steps, forward_step, 0)
+    for r in range(n_z):
+        sums_ref[r] = sums_acc[:, r * part : (r + 1) * part].astype(BF)
 
     def sums_copy(d):
         z = lax.rem(q + d, n_z)
@@ -291,23 +323,12 @@
 
     for d in range(1, n_z):
         sums_copy(d).start()
-    agg_copy = remote(
-        agg_hbm.at[pl.ds((1 - core) * half, half)],
-        agg_sib,
-        agg_send,
-        agg_recv,
-        q,
-        sib,
-    )
-    agg_copy.start()
-    pick[...] = one_hot(pick.shape[0], dst_ref[...])
-    pick_src[...] = one_hot(pick.shape[0], src_ref[...])
     total = sums_ref[q].astype(F32)
     for d in range(1, n_z):
         sums_wait(d)
         total += sums_in[lax.rem(q + d, n_z)].astype(F32)
     inverse = inv_ref[...]
-    pre = pre + total * inverse
+    pre = pre_self[...] + total * inverse
     sig = jax.nn.sigmoid(pre)
     slope = sig * (1.0 + pre * (1.0 - sig))
     pre_in[q] = (cot_ref[:, lanes].astype(F32) * slope).astype(BF)
@@ -336,12 +357,10 @@
     grad = dot(pre_in[0], w_rows[:, :part], ((1,), (1,)))
     for z in range(1, n_z):
         grad += dot(pre_in[z], w_rows[:, z * part : (z + 1) * part], ((1,), (1,)))
-    load_agg.wait()
     agg_copy.wait_recv()
     sib_copy.wait_recv()
 
     group = 4
-    n_ent = agg_own.shape[2]
     wide = width // 2
 
     def x_first(d, slot):
@@ -370,7 +389,7 @@
 
     for d in (2, 1, 3, 0):
         at = lax.rem(x + d, 4)
-        own = agg_own[pl.ds(at * group, group)].reshape(group * part, n_ent)
+        own = agg[pl.ds(core * half + at * group, group)].reshape(group * part, n_ent)
         other = agg_sib[pl.ds(at * group, group)].reshape(group * part, n_ent)
         terms = dot(own, scaled[...]) + dot(other, scaled_sib[...])
         terms = terms.astype(BF)
@@ -383,8 +402,6 @@
         y_first(d, y).start()
     for d in range(1, n_z):
         act_copy(d, q).start()
-    for load in loads:
-        load.wait()
     seg = acc.shape[1]
 
     def back_step(i, _):
@@ -423,11 +440,6 @@
 
         return 0
 
-    def row_wait(d, _):
-        peer = lax.rem(e + d, n_e)
-        row_copy(peer, peer).wait_recv()
-        return 0
-
     per_seg = n_e * seg // pick.shape[1]
     for n in range(n_e // per_seg):
         spread(n * seg)
@@ -448,7 +460,7 @@
     half_y[...] = add_up(term_y[y], y_in, y_first, y).astype(BF)
     for d in (2, 1, 3):
         y_then_x(d, x).start()
-    lax.fori_loop(1, n_e, row_wait, 0)
+    wait_all(row_copy)
     grad += dot(pick_src[...], row_in[...].reshape(pick_src.shape[1], part))
     gf_ref[:, lanes] = grad.astype(BF)
 
@@ -493,39 +505,53 @@
         x_then_y(d, y).wait_send()
         y_then_x(d, x).wait_send()
 
-    def row_sent(d, _):
-        row_copy(lax.rem(e + d, n_e), e).wait_send()
-        return 0
-
-    lax.fori_loop(1, n_e, row_sent, 0)
-
-
-def finish(sums, inverse, features, w_self, cotangent, src, dst, coef_t, agg, basis_mats):
+    for d in range(1, n_z):
+        meta_copy(d, q).wait_send()
+    sent_all(tag_copy)
+    sent_all(feed_copy)
+    sent_all(row_copy)
+
+
+def run_step(meta, features, w_self, cotangent, coeffs, basis_mats):
     n_z = lax.axis_size("rel")
     n_e = lax.axis_size("ent")
     n_ent, width = features.shape
-    bases, all_slots = coef_t.shape
+    bases = coeffs.shape[1]
+    all_slots = meta.shape[0] * meta.shape[3]
     part = width // n_z
     half = bases // 2
     block = all_slots // n_e
     vm = pl.BlockSpec(memory_space=pltpu.VMEM)
-    hbm = pl.BlockSpec(memory_space=pl.ANY)
     dma = pltpu.SemaphoreType.DMA
     return pl.pallas_call(
-        functools.partial(finish_kernel, n_z, n_e),
+        functools.partial(step_kernel, n_z, n_e),
         out_shape=(
             jax.ShapeDtypeStruct((n_ent, width), BF),
             jax.ShapeDtypeStruct((n_ent, width), BF),
             jax.ShapeDtypeStruct((part, width), F32),
         ),
-        in_specs=[vm] * 8 + [hbm, hbm],
+        in_specs=[vm] * 5 + [pl.BlockSpec(memory_space=pl.ANY)],
         out_specs=(vm, vm, vm),
         scratch_shapes=[
+            pltpu.VMEM((n_z,) + meta.shape, I32),
+            pltpu.VMEM(meta.shape, I32),
+            pltpu.VMEM((n_e,) + meta.shape[1:], I32),
+            pltpu.VMEM((1, all_slots), I32),
+            pltpu.VMEM((1, all_slots), I32),
+            pltpu.VMEM((1024, 128), F32),
+            pltpu.VMEM((n_e, block, part), BF),
+            pltpu.VMEM((n_e, block, part), BF),
+            pltpu.VMEM((part, all_slots), F32),
+            pltpu.VMEM((bases, all_slots), F32),
+            pltpu.VMEM((n_ent, part), F32),
+            pltpu.VMEM((n_ent, part), F32),
+            pltpu.VMEM((n_ent, width), F32),
+            pltpu.VMEM((n_z, n_ent, part), BF),
+            pltpu.VMEM((bases, part, n_ent), BF),
             pltpu.VMEM((n_z, n_ent, part), BF),
             pltpu.VMEM((n_z, n_ent, part), BF),
             pltpu.VMEM((n_ent, width), BF),
             pltpu.VMEM((n_ent, width), BF),
-            pltpu.VMEM((half, part, n_ent), BF),
             pltpu.VMEM((half, part, n_ent), BF),
             pltpu.VMEM((bases, part, width), BF),
             pltpu.VMEM((n_ent, all_slots), BF),
@@ -544,7 +570,6 @@
             pltpu.VMEM((n_e, block, part), BF),
             pltpu.VMEM((n_e, block, part), BF),
             dma((bases // 4,)),
-            dma,
             dma((n_z,)),
             dma((n_z,)),
             dma((n_z,)),
@@ -569,20 +594,22 @@
             dma((n_e,)),
             dma((n_z,)),
             dma((n_z,)),
+            dma((n_z,)),
+            dma((n_z,)),
+            dma((n_e,)),
+            dma((n_e,)),
+            dma((n_e,)),
+            dma((n_e,)),
         ],
         compiler_params=pltpu.CompilerParams(
             vmem_limit_bytes=56 * MIB, collective_id=0, has_side_effects=True
         ),
     )(
-        sums,
-        inverse,
+        meta,
         features,
         w_self,
         cotangent,
-        src,
-        dst,
-        coef_t,
-        agg,
+        coeffs,
         basis_mats.reshape(2, 2, 4, 2, width, width),
     )
 
@@ -604,11 +631,8 @@
     rel_count = lax.axis_size("rel")
     slots = rel_local.shape[0]
     cap = slots // ent_count
-    bases = basis_coeffs.shape[1]
-    part = width // rel_count
     q = lax.axis_index("rel")
     s = lax.axis_index("ent")
-    all_slots = slots * rel_count
 
     shape = (ent_count, cap)
     live = lax.broadcasted_iota(I32, shape, 1) < block_counts.reshape(ent_count, 1)
@@ -619,23 +643,11 @@
     rel_own = jnp.sum(
         jnp.where(rel_local[:, None] == ids[None, :], group_rels[None, :], 0), axis=1
     ).reshape(shape)
-    meta = jnp.stack([src_own, dst_own, rel_own])
-    meta = lax.all_gather(meta, "rel")
-    meta = meta.transpose(2, 1, 0, 3)
-    src = meta[:, 0].reshape(1, all_slots)
-    arrived = swap(meta[:, 1:], "ent")
-    dst = arrived[:, 0].reshape(1, all_slots)
-    rel = arrived[:, 1].reshape(1, all_slots)
-
-    pick_src = (jnp.arange(n_ent, dtype=I32)[:, None] == src).astype(BF)
-    feat_part = lax.dynamic_slice_in_dim(features, q * part, part, 1)
-    rows = dot(pick_src, feat_part, ((0,), (0,))).astype(BF)
-    rows = swap(rows.reshape(ent_count, rel_count * cap, part), "ent").reshape(all_slots, part)
-
-    partial, agg, inverse, coef_t = forward(dst, rel, rows, basis_coeffs, basis_mats, n_ent)
-    return finish(
-        partial, inverse, features, w_self, cotangent, src, dst, coef_t, agg, basis_mats
-    )
+    meta = jnp.stack([src_own, dst_own, rel_own]).reshape(3, ent_count // 2, 2, 1, cap)
+    mine = jnp.arange(rel_count, dtype=I32)[:, None] == q
+    meta = jnp.where(mine, meta, 0).transpose(1, 0, 2, 3, 4)
+    meta = meta.reshape(ent_count // 2, 3, 1, 2 * rel_count * cap)
+    return run_step(meta, features, w_self, cotangent, basis_coeffs, basis_mats)
 
 
 def solution(mesh):

time: 149 us -> 120 us (0.81)
  starting transfers between devices: 16.2 us -> 0 us
  blocking collectives: 10.6 us -> 0 us
  Pallas kernels: 95.7 us -> 106 us
  waiting for transfers between devices: 6.56 us -> 0 us
  local copies, waits for them, and re-layouts: 12.6 us -> 9.22 us
  matrix products: 2.98 us -> 0 us
    all_to_all x2 -> x0, starting transfers between devices: 16.2 us -> none  [swap(): return lax.all_to_all(x, axis, split_axis=0, concat_axis=0, tiled=True)]
    all_gather x1 -> x0, blocking collectives: 10.6 us -> none  [per_device(): meta = lax.all_gather(meta, 'rel')]
    pallas_call x2 -> x1, Pallas kernels: 95.7 us -> 106 us  [run_step(): pl.pallas_call(functools.partial(step_kernel, n_z, n_e), out_shape=(jax.S...]
    all_to_all x2 -> x0, waiting for transfers between devices: 6.56 us -> none  [swap(): return lax.all_to_all(x, axis, split_axis=0, concat_axis=0, tiled=True)]
    dot_general x1 -> x0, matrix products: 2.98 us -> none  [dot(): return lax.dot_general(a, b, (dims, ((), ())), preferred_element_type=F32)]
    another operation x5 -> x1, local copies, waits for them, and re-layouts: 2.26 us -> 0.09 us  [per_device(): jnp.stack([src_own, dst_own, rel_own]).reshape(3, ent_count // 2, 2, 1, cap)]
    unnamed x10 -> x5, local copies, waits for them, and re-layouts: 8.22 us -> 7.81 us
  transfers between devices with their start and end apart: 2 -> 0, of which waited for: 2 -> 0; matrix products, arithmetic and copies ran while one was open for 5% -> 0% of each run, Pallas kernels for 0% -> 0%
where the time goes in v5:
time: 120 us
  Pallas kernels  106 us (88%)
  local copies, waits for them, and re-layouts  9.22 us (8%)
  other arithmetic  3.7 us (3%)
    pallas_call x1, Pallas kernels, run_step(): pl.pallas_call(functools.partial(step_kernel, n_z, n_e), out_shape=(jax.S...  106 us
    unnamed x5, local copies, waits for them, and re-layouts  7.81 us

profile of v5, /device:TPU:25, one launch (start us, length us, event | category | flops | bytes accessed | tf_op | source)
XLA Modules:
  0.0 120.0 jit_solution(210525123222684111)
XLA Ops:
  0.6 0.5 broadcast.72
  1.2 1.3 %reduce.3 = s32[32]{0:T(128)S(1)} reduce(s32[1,1,32]{2,1,0:T(1,128)} %param.18, s32[]{:T(128)} %broadcast.72), dimensions={0,1}, to_apply=%param.18.reduce_sub_computation.3 | reduce | bytes 260 | tf_op args[8]
  2.5 0.1 broadcast_in_dim.48
  2.6 0.1 broadcast_in_dim.49
  2.6 0.7 broadcast_subtract_fusion
  3.3 0.9 select_reduce_fusion
  4.3 0.1 lt.18
  4.4 0.1 stack.7
  4.5 0.1 sub.30
  4.5 0.8 reshape.91
  5.3 0.1 compare_select_fusion
  5.5 0.2 broadcast_in_dim.56
  5.7 0.6 broadcast_select_fusion.meta_ref
  6.3 1.9 %copy.15.coef_ref = f32[1000,32]{1,0:T(8,128)} copy(f32[1000,32]{0,1:T(8,128)} %param.13) | data formatting | bytes 256000 | tf_op args[3]
  8.2 106.3 %shard_map.121 = (bf16[512,512]{1,0:T(8,128)(2,1)}, bf16[512,512]{1,0:T(8,128)(2,1)}, f32[128,512]{1,0:T(8,128)}) custom-call(s32[16,3,1,128]{3,2,1,0:T(1,128)} %broadcast_select_fusion.meta_ref, bf16[512,512]{1,0:T(8,128)(2,1)} %feat_ref.1, bf16[512,512]{1,0:T(8,128)(2,1)} %w_ref.1, bf16[512,512]{1,0:T(8,128)(2,1)} %cot_ref.1, f32[1000,32]{1,0:T(8,128)} %copy.15.coef_ref, ...), custom_call_target="tpu_custom_call" | custom-call | tf_op jit(solution)/shard_map/pallas_call | solution.py:526
  114.6 1.9 %copy.19 = bf16[512,512]{1,0:T(8,128)(2,1)} copy(bf16[512,512]{1,0:T(8,128)(2,1)} %get-tuple-element.6) | data formatting | bytes 1048576
  116.4 1.9 %copy.20 = bf16[512,512]{1,0:T(8,128)(2,1)} copy(bf16[512,512]{1,0:T(8,128)(2,1)} %get-tuple-element.7) | data formatting | bytes 1048576
  118.3 1.7 %copy.21 = f32[128,512]{1,0:T(8,128)} copy(f32[128,512]{1,0:T(8,128)} %get-tuple-element.8) | data formatting | bytes 524288
  (4 shorter events, 0.1 us)

commit v6 on v5

--- a/solution.py
+++ b/solution.py
@@ -68,10 +68,51 @@
     )
 
 
+def place_metadata(q, e, src_ref, dst_ref, rel_ref, group_row, counts_ref, meta_ref, n_ent):
+    slots = src_ref.shape[1]
+    n_e = counts_ref.shape[1]
+    pairs, fields, _, lanes = meta_ref.shape
+    cap = slots // n_e
+    spot = lax.broadcasted_iota(I32, (1, slots), 1)
+    peer = lax.div(spot, cap)
+    rows16 = lax.broadcasted_iota(I32, (pairs, slots), 0)
+
+    def digits(v):
+        return lax.div(v, 32).astype(F32), lax.rem(v, 32).astype(F32)
+
+    hi, lo = digits(group_row[...])
+    level = lax.broadcasted_iota(I32, (pairs, group_row.shape[1]), 0)
+    table = jnp.where(level == 0, hi, jnp.where(level == 1, lo, 0.0)).astype(BF)
+    rel_digits = dot(table, one_hot(group_row.shape[1], rel_ref[...]))
+    counts = jnp.broadcast_to(counts_ref[...].astype(F32), (pairs, n_e)).astype(BF)
+    limit = dot(counts, one_hot(n_e, peer))[:1]
+    live = lax.rem(spot, cap).astype(F32) < limit
+    dst = jnp.where(live, dst_ref[...] - peer * n_ent, n_ent)
+    values = digits(src_ref[...] - e * n_ent) + digits(dst)
+    values = values + (rel_digits[:1], rel_digits[1:2])
+    here = rows16 == lax.div(peer, 2)
+    stacked = jnp.concatenate([jnp.where(here, v, 0.0) for v in values], axis=0).astype(BF)
+    index = lax.broadcasted_iota(I32, (slots, lanes), 0)
+    lane = lax.broadcasted_iota(I32, (slots, lanes), 1)
+    half = lax.rem(lax.div(index, cap), 2)
+    target = half * (lanes // 2) + q * cap + lax.rem(index, cap)
+    moved = dot(stacked, (target == lane).astype(F32).astype(BF))
+    for f in range(fields):
+        hi = moved[2 * f * pairs : (2 * f + 1) * pairs]
+        lo = moved[(2 * f + 1) * pairs : (2 * f + 2) * pairs]
+        field = (hi * 32.0 + lo + 0.5).astype(I32)
+        for t in range(pairs):
+            meta_ref[t, f] = field[t : t + 1, :]
+
+
 def step_kernel(
     n_z,
     n_e,
-    meta_ref,
+    src_ref,
+    dst_ref,
+    rel_ref,
+    groups_ref,
+    counts_ref,
     feat_ref,
     w_ref,
     cot_ref,
@@ -80,6 +121,8 @@
     act_ref,
     gf_ref,
     gb_ref,
+    group_row,
+    meta_ref,
     meta_z,
     meta_all,
     tags,
@@ -193,7 +236,12 @@
     for load in loads:
         load.start()
     table[...] = jnp.zeros_like(table)
-    table[: coef_ref.shape[0], :bases] = coef_ref[...]
+    table[:, : coef_ref.shape[1]] = coef_ref[...]
+    group_row[...] = jnp.zeros_like(group_row)
+    group_row[:, : groups_ref.shape[1]] = groups_ref[...]
+    place_metadata(
+        q, e, src_ref, dst_ref, rel_ref, group_row, counts_ref, meta_ref, feat_ref.shape[0]
+    )
     pre_self[...] = dot(feat_ref[...], w_ref[:, lanes])
     pl.semaphore_wait(barrier, n_z - 1 + n_e - 1 + moves.astype(I32))
 
@@ -268,10 +316,10 @@
             even = jnp.where(core == 0, even, pltpu.roll(even, wide_lanes // 2, 1))
             odd = jnp.where(core == 0, pltpu.roll(odd, wide_lanes // 2, 1), odd)
             out[:, t * wide_lanes : (t + 1) * wide_lanes] = jnp.where(left, even, odd)
-    which = one_hot(table.shape[0], line_rel[...])
+    which = one_hot(table.shape[1], line_rel[...])
     hi, mid, lo = split3(table[...])
-    coef_t = dot(hi, which, ((0,), (0,))) + dot(mid, which, ((0,), (0,)))
-    coef_t = coef_t + dot(lo, which, ((0,), (0,)))
+    coef_t = dot(jnp.concatenate([hi, mid, lo], axis=0), which)
+    coef_t = coef_t[:bases] + coef_t[bases : 2 * bases] + coef_t[2 * bases : 3 * bases]
     for p, b in enumerate(slot_order(bases)):
         coef_t_ref[p : p + 1, :] = coef_t[b : b + 1, :]
     pick[...] = one_hot(n_ent, line[...])
@@ -512,12 +560,12 @@
     sent_all(row_copy)
 
 
-def run_step(meta, features, w_self, cotangent, coeffs, basis_mats):
+def run_step(src, dst, rel, groups, counts, features, w_self, cotangent, coeffs, basis_mats):
     n_z = lax.axis_size("rel")
     n_e = lax.axis_size("ent")
     n_ent, width = features.shape
-    bases = coeffs.shape[1]
-    all_slots = meta.shape[0] * meta.shape[3]
+    bases = coeffs.shape[0]
+    all_slots = src.shape[1] * n_z
     part = width // n_z
     half = bases // 2
     block = all_slots // n_e
@@ -530,15 +578,17 @@
             jax.ShapeDtypeStruct((n_ent, width), BF),
             jax.ShapeDtypeStruct((part, width), F32),
         ),
-        in_specs=[vm] * 5 + [pl.BlockSpec(memory_space=pl.ANY)],
+        in_specs=[vm] * 9 + [pl.BlockSpec(memory_space=pl.ANY)],
         out_specs=(vm, vm, vm),
         scratch_shapes=[
-            pltpu.VMEM((n_z,) + meta.shape, I32),
-            pltpu.VMEM(meta.shape, I32),
-            pltpu.VMEM((n_e,) + meta.shape[1:], I32),
+            pltpu.VMEM((1, 256), I32),
+            pltpu.VMEM((n_e // 2, 3, 1, 128), I32),
+            pltpu.VMEM((n_z, n_e // 2, 3, 1, 128), I32),
+            pltpu.VMEM((n_e // 2, 3, 1, 128), I32),
+            pltpu.VMEM((n_e, 3, 1, 128), I32),
             pltpu.VMEM((1, all_slots), I32),
             pltpu.VMEM((1, all_slots), I32),
-            pltpu.VMEM((1024, 128), F32),
+            pltpu.VMEM((bases, 1024), F32),
             pltpu.VMEM((n_e, block, part), BF),
             pltpu.VMEM((n_e, block, part), BF),
             pltpu.VMEM((part, all_slots), F32),
@@ -605,13 +655,39 @@
             vmem_limit_bytes=56 * MIB, collective_id=0, has_side_effects=True
         ),
     )(
-        meta,
+        src,
+        dst,
+        rel,
+        groups,
+        counts,
         features,
         w_self,
         cotangent,
         coeffs,
         basis_mats.reshape(2, 2, 4, 2, width, width),
     )
+
+
+def store_kernel(a_in, b_in, c_in, a_out, b_out, c_out, sems):
+    copies = [
+        pltpu.make_async_copy(i, o, sems.at[n])
+        for n, (i, o) in enumerate(((a_in, a_out), (b_in, b_out), (c_in, c_out)))
+    ]
+    for copy in copies:
+        copy.start()
+    for copy in copies:
+        copy.wait()
+
+
+def store(arrays):
+    hbm = pl.BlockSpec(memory_space=pl.ANY)
+    return pl.pallas_call(
+        store_kernel,
+        out_shape=tuple(jax.ShapeDtypeStruct(a.shape, a.dtype) for a in arrays),
+        in_specs=[hbm] * 3,
+        out_specs=(hbm,) * 3,
+        scratch_shapes=[pltpu.SemaphoreType.DMA((3,))],
+    )(*arrays)
 
 
 def per_device(
@@ -626,28 +702,19 @@
     block_counts,
     cotangent,
 ):
-    n_ent, width = features.shape
-    ent_count = lax.axis_size("ent")
-    rel_count = lax.axis_size("rel")
-    slots = rel_local.shape[0]
-    cap = slots // ent_count
-    q = lax.axis_index("rel")
-    s = lax.axis_index("ent")
-
-    shape = (ent_count, cap)
-    live = lax.broadcasted_iota(I32, shape, 1) < block_counts.reshape(ent_count, 1)
-    src_own = edge_src.reshape(shape) - s * n_ent
-    base = lax.broadcasted_iota(I32, shape, 0) * n_ent
-    dst_own = jnp.where(live, edge_dst.reshape(shape) - base, n_ent)
-    ids = jnp.arange(group_rels.shape[0], dtype=I32)
-    rel_own = jnp.sum(
-        jnp.where(rel_local[:, None] == ids[None, :], group_rels[None, :], 0), axis=1
-    ).reshape(shape)
-    meta = jnp.stack([src_own, dst_own, rel_own]).reshape(3, ent_count // 2, 2, 1, cap)
-    mine = jnp.arange(rel_count, dtype=I32)[:, None] == q
-    meta = jnp.where(mine, meta, 0).transpose(1, 0, 2, 3, 4)
-    meta = meta.reshape(ent_count // 2, 3, 1, 2 * rel_count * cap)
-    return run_step(meta, features, w_self, cotangent, basis_coeffs, basis_mats)
+    outs = run_step(
+        edge_src[None],
+        edge_dst[None],
+        rel_local[None],
+        group_rels[None],
+        block_counts[0],
+        features,
+        w_self,
+        cotangent,
+        basis_coeffs.T,
+        basis_mats,
+    )
+    return store(outs)
 
 
 def solution(mesh):

time: 120 us -> 148 us (1.23)
  Pallas kernels: 106 us -> 147 us
  local copies, waits for them, and re-layouts: 9.22 us -> 0 us
  other arithmetic: 3.7 us -> 0 us
    pallas_call x0 -> x1, Pallas kernels: none -> 40.8 us  [store(): pl.pallas_call(store_kernel, out_shape=tuple((jax.ShapeDtypeStruct(a.shap...]
    unnamed x5 -> x0, local copies, waits for them, and re-layouts: 7.81 us -> none
where the time goes in v6:
time: 148 us
  Pallas kernels  147 us (99%)
    pallas_call x1, Pallas kernels, run_step(): pl.pallas_call(functools.partial(step_kernel, n_z, n_e), out_shape=(jax.S...  106 us
    pallas_call x1, Pallas kernels, store(): pl.pallas_call(store_kernel, out_shape=tuple((jax.ShapeDtypeStruct(a.shap...  40.8 us

profile of v6, /device:TPU:25, one launch (start us, length us, event | category | flops | bytes accessed | tf_op | source)
XLA Modules:
  0.0 147.6 jit_solution(2503410813380088680)
XLA Ops:
  0.6 106.1 %shard_map.121 = (bf16[512,512]{1,0:T(8,128)(2,1)}, bf16[512,512]{1,0:T(8,128)(2,1)}, f32[128,512]{1,0:T(8,128)}) custom-call(s32[1,512]{1,0:T(1,128)} %bitcast.9, s32[1,512]{1,0:T(1,128)} %bitcast.10, s32[1,512]{1,0:T(1,128)} %bitcast.11, s32[1,250]{1,0:T(1,128)} %bitcast.12, s32[1,32]{1,0:T(1,128)} %bitcast.13, bf16[512,512]{1,0:T(8,128)(2,1)} %feat_ref.1, ...), custom_call_target="tpu_custom_call" | custom-call | tf_op jit(solution)/shard_map/pallas_call | solution.py:574
  106.7 40.8 %shard_map.122 = (bf16[512,512]{1,0:T(8,128)(2,1)}, bf16[512,512]{1,0:T(8,128)(2,1)}, f32[128,512]{1,0:T(8,128)}) custom-call(bf16[512,512]{1,0:T(8,128)(2,1)} %get-tuple-element.6.a_in, bf16[512,512]{1,0:T(8,128)(2,1)} %get-tuple-element.7.b_in, f32[128,512]{1,0:T(8,128)} %get-tuple-element.8.c_in), custom_call_target="tpu_custom_call" | custom-call | tf_op jit(solution)/shard_map/pallas_call | solution.py:684

commit v7 on v6

--- a/solution.py
+++ b/solution.py
@@ -330,7 +330,7 @@
     rows_t[...] = feed_in[...].reshape(pick.shape[1], part).astype(F32).T
     for load in loads:
         load.wait()
-    pair = 2
+    pair = 8
 
     def forward_step(i, _):
         at = i * pair
@@ -684,7 +684,7 @@
     return pl.pallas_call(
         store_kernel,
         out_shape=tuple(jax.ShapeDtypeStruct(a.shape, a.dtype) for a in arrays),
-        in_specs=[hbm] * 3,
+        in_specs=[pl.BlockSpec(memory_space=pltpu.VMEM)] * 3,
         out_specs=(hbm,) * 3,
         scratch_shapes=[pltpu.SemaphoreType.DMA((3,))],
     )(*arrays)

time: 148 us -> 103 us (0.70)
  Pallas kernels: 147 us -> 102 us
    pallas_call x1, Pallas kernels: 40.8 us -> 2.34 us  [store(): pl.pallas_call(store_kernel, out_shape=tuple((jax.ShapeDtypeStruct(a.shap...]
    pallas_call x1, Pallas kernels: 106 us -> 99.5 us  [run_step(): pl.pallas_call(functools.partial(step_kernel, n_z, n_e), out_shape=(jax.S...]
where the time goes in v7:
time: 103 us
  Pallas kernels  102 us (99%)
    pallas_call x1, Pallas kernels, run_step(): pl.pallas_call(functools.partial(step_kernel, n_z, n_e), out_shape=(jax.S...  99.5 us
    pallas_call x1, Pallas kernels, store(): pl.pallas_call(store_kernel, out_shape=tuple((jax.ShapeDtypeStruct(a.shap...  2.34 us

profile of v7, /device:TPU:25, one launch (start us, length us, event | category | flops | bytes accessed | tf_op | source)
XLA Modules:
  0.0 102.7 jit_solution(17089378894905358316)
XLA Ops:
  0.6 99.5 %shard_map.121 = (bf16[512,512]{1,0:T(8,128)(2,1)}, bf16[512,512]{1,0:T(8,128)(2,1)}, f32[128,512]{1,0:T(8,128)}) custom-call(s32[1,512]{1,0:T(1,128)} %bitcast.9, s32[1,512]{1,0:T(1,128)} %bitcast.10, s32[1,512]{1,0:T(1,128)} %bitcast.11, s32[1,250]{1,0:T(1,128)} %bitcast.12, s32[1,32]{1,0:T(1,128)} %bitcast.13, bf16[512,512]{1,0:T(8,128)(2,1)} %feat_ref.1, ...), custom_call_target="tpu_custom_call" | custom-call | tf_op jit(solution)/shard_map/pallas_call | solution.py:574
  100.2 2.3 %shard_map.122 = (bf16[512,512]{1,0:T(8,128)(2,1)}, bf16[512,512]{1,0:T(8,128)(2,1)}, f32[128,512]{1,0:T(8,128)}) custom-call(bf16[512,512]{1,0:T(8,128)(2,1)} %get-tuple-element.6.a_in, bf16[512,512]{1,0:T(8,128)(2,1)} %get-tuple-element.7.b_in, f32[128,512]{1,0:T(8,128)} %get-tuple-element.8.c_in), custom_call_target="tpu_custom_call" | custom-call | tf_op jit(solution)/shard_map/pallas_call | solution.py:684

commit v8 on v7

--- a/solution.py
+++ b/solution.py
@@ -157,6 +157,7 @@
     xy_in,
     yx_in,
     done,
+    done_in,
     row_out,
     row_in,
     basis_sem,
@@ -331,59 +332,88 @@
     for load in loads:
         load.wait()
     pair = 8
-
-    def forward_step(i, _):
-        at = i * pair
-        mixed = jnp.concatenate(
-            [
-                (rows_t[...] * coef_t_ref[pl.ds(at + g, 1), :]).astype(BF)
-                for g in range(pair)
-            ],
-            axis=0,
-        )
-        out = dot(pick[...], mixed, ((1,), (1,)))
-        weights = basis[pl.ds(at, pair)].reshape(pair * part, width)
-        sums_acc[...] += dot(out.astype(BF), weights)
-        agg[pl.ds(at, pair)] = out.T.astype(BF).reshape(pair, part, n_ent)
-        return 0
+    chunk = n_ent // 2
+    steps = bases // pair
+
+    def forward_half(h, first, last):
+        rows = pl.ds(h * chunk, chunk)
+
+        def forward_step(i, _):
+            at = i * pair
+            mixed = jnp.concatenate(
+                [
+                    (rows_t[...] * coef_t_ref[pl.ds(at + g, 1), :]).astype(BF)
+                    for g in range(pair)
+                ],
+                axis=0,
+            )
+            out = dot(pick[rows, :], mixed, ((1,), (1,)))
+            weights = basis[pl.ds(at, pair)].reshape(pair * part, width)
+            sums_acc[rows, :] += dot(out.astype(BF), weights)
+            agg[pl.ds(at, pair), :, rows] = out.T.astype(BF).reshape(pair, part, chunk)
+            return 0
+
+        lax.fori_loop(first, last, forward_step, 0)
 
     agg_copy = remote(
         agg.at[pl.ds((1 - core) * half, half)], agg_sib, agg_send, agg_recv, q, sib
     )
-    steps = half // pair
-    lax.fori_loop((1 - core) * steps, (2 - core) * steps, forward_step, 0)
+
+    def sums_copy(d, slot, h):
+        z = lax.rem(q + d, n_z)
+        at = pl.ds(h * chunk, chunk)
+        return remote(
+            sums_ref.at[z, at],
+            sums_in.at[slot, at],
+            sums_send.at[d, h],
+            sums_recv.at[slot, h],
+            z,
+            e,
+        )
+
+    def pre_copy(d, slot, h):
+        z = lax.rem(q + d, n_z)
+        at = pl.ds(h * chunk, chunk)
+        return remote(
+            pre_in.at[q, at], pre_in.at[slot, at], pre_send.at[d, h], pre_recv.at[slot, h], z, e
+        )
+
+    def sib_copy(h):
+        at = pl.ds(h * chunk, chunk)
+        return remote(
+            scaled.at[at], scaled_sib.at[at], sib_send.at[h], sib_recv.at[h], q, sib
+        )
+
+    def send_sums(h):
+        at = pl.ds(h * chunk, chunk)
+        for r in range(n_z):
+            sums_ref[r, at] = sums_acc[at, r * part : (r + 1) * part].astype(BF)
+        for d in range(1, n_z):
+            sums_copy(d, q, h).start()
+
+    def activate(h):
+        at = pl.ds(h * chunk, chunk)
+        total = sums_ref[q, at].astype(F32)
+        for d in range(1, n_z):
+            slot = lax.rem(q + d, n_z)
+            sums_copy(d, slot, h).wait_recv()
+            total += sums_in[slot, at].astype(F32)
+        pre = pre_self[at] + total * inv_ref[at]
+        sig = jax.nn.sigmoid(pre)
+        slope = sig * (1.0 + pre * (1.0 - sig))
+        pre_in[q, at] = (cot_ref[at, lanes].astype(F32) * slope).astype(BF)
+        for d in range(1, n_z):
+            pre_copy(d, q, h).start()
+        act_ref[at, lanes] = (pre * sig).astype(BF)
+
+    forward_half(0, 0, steps)
+    send_sums(0)
+    forward_half(1, 0, steps - 1)
+    activate(0)
+    forward_half(1, steps - 1, steps)
+    send_sums(1)
     agg_copy.start()
-    lax.fori_loop(core * steps, (1 + core) * steps, forward_step, 0)
-    for r in range(n_z):
-        sums_ref[r] = sums_acc[:, r * part : (r + 1) * part].astype(BF)
-
-    def sums_copy(d):
-        z = lax.rem(q + d, n_z)
-        return remote(
-            sums_ref.at[z], sums_in.at[q], sums_send.at[d], sums_recv.at[q], z, e
-        )
-
-    def sums_wait(d):
-        z = lax.rem(q + d, n_z)
-        remote(
-            sums_ref.at[z], sums_in.at[z], sums_send.at[d], sums_recv.at[z], z, e
-        ).wait_recv()
-
-    for d in range(1, n_z):
-        sums_copy(d).start()
-    total = sums_ref[q].astype(F32)
-    for d in range(1, n_z):
-        sums_wait(d)
-        total += sums_in[lax.rem(q + d, n_z)].astype(F32)
-    inverse = inv_ref[...]
-    pre = pre_self[...] + total * inverse
-    sig = jax.nn.sigmoid(pre)
-    slope = sig * (1.0 + pre * (1.0 - sig))
-    pre_in[q] = (cot_ref[:, lanes].astype(F32) * slope).astype(BF)
-
-    def pre_copy(d, z_in):
-        z = lax.rem(q + d, n_z)
-        return remote(pre_in.at[q], pre_in.at[z_in], pre_send.at[d], pre_recv.at[z_in], z, e)
+    activate(1)
 
     def act_copy(d, z_in):
         z = lax.rem(q + d, n_z)
@@ -392,23 +422,31 @@
             act_ref.at[:, lanes], act_ref.at[:, at], act_send.at[d], act_recv.at[z_in], z, e
         )
 
-    for d in range(1, n_z):
-        pre_copy(d, q).start()
-    act_ref[:, lanes] = (pre * sig).astype(BF)
-    for d in range(1, n_z):
-        pre_copy(d, lax.rem(q + d, n_z)).wait_recv()
-    for z in range(n_z):
-        scaled[:, z * part : (z + 1) * part] = (pre_in[z].astype(F32) * inverse).astype(BF)
-    sib_copy = remote(scaled, scaled_sib, sib_send, sib_recv, q, sib)
-    sib_copy.start()
+    for h in range(2):
+        at = pl.ds(h * chunk, chunk)
+        for d in range(1, n_z):
+            pre_copy(d, lax.rem(q + d, n_z), h).wait_recv()
+        inverse = inv_ref[at]
+        for z in range(n_z):
+            part_in = pre_in[z, at].astype(F32) * inverse
+            scaled[at, z * part : (z + 1) * part] = part_in.astype(BF)
+        sib_copy(h).start()
     w_rows = w_ref[lanes, :]
     grad = dot(pre_in[0], w_rows[:, :part], ((1,), (1,)))
     for z in range(1, n_z):
         grad += dot(pre_in[z], w_rows[:, z * part : (z + 1) * part], ((1,), (1,)))
+    group = 4
+
+    def back_step(i, _):
+        weights = basis[pl.ds(i * group, group)].reshape(group * part, width)
+        back[i] = dot(weights, scaled[...], ((1,), (1,))).astype(BF)
+        return 0
+
+    lax.fori_loop(0, bases // group, back_step, 0)
+
     agg_copy.wait_recv()
-    sib_copy.wait_recv()
-
-    group = 4
+    for h in range(2):
+        sib_copy(h).wait_recv()
     wide = width // 2
 
     def x_first(d, slot):
@@ -452,13 +490,6 @@
         act_copy(d, q).start()
     seg = acc.shape[1]
 
-    def back_step(i, _):
-        weights = basis[pl.ds(i * group, group)].reshape(group * part, width)
-        back[i] = dot(weights, scaled[...], ((1,), (1,))).astype(BF)
-        return 0
-
-    lax.fori_loop(0, bases // group, back_step, 0)
-
     def spread(first):
         acc[...] = jnp.zeros_like(acc)
 
@@ -522,30 +553,34 @@
     for d in range(1, n_z):
         gf_copy(d, q).start()
 
-    done[:, :wide] = add_up(half_x[y], xy_in, x_then_y, y)
-    done[:, wide:] = add_up(half_y[x], yx_in, y_then_x, x)
-    move = remote(done, gb_ref, move_send, move_recv, to_z, to_e)
+    done[:, :wide] = add_up(half_x[y], xy_in, x_then_y, y).astype(BF)
+    done[:, wide:] = add_up(half_y[x], yx_in, y_then_x, x).astype(BF)
+    move = remote(done, done_in, move_send, move_recv, to_z, to_e)
 
     @pl.when(keeps)
     def _():
-        gb_ref[...] = done[...]
+        done_in[...] = done[...]
 
     @pl.when(moves)
     def _():
         move.start()
         move.wait_send()
-        remote(done, gb_ref, move_send, move_recv, from_z, from_e).wait_recv()
+        remote(done, done_in, move_send, move_recv, from_z, from_e).wait_recv()
+
+    gb_ref[...] = done_in[...].astype(F32)
 
     for d in range(1, n_z):
         z = lax.rem(q + d, n_z)
         act_copy(d, z).wait_recv()
         gf_copy(d, z).wait_recv()
-        sums_copy(d).wait_send()
-        pre_copy(d, q).wait_send()
+        for h in range(2):
+            sums_copy(d, q, h).wait_send()
+            pre_copy(d, q, h).wait_send()
         act_copy(d, q).wait_send()
         gf_copy(d, q).wait_send()
     agg_copy.wait_send()
-    sib_copy.wait_send()
+    for h in range(2):
+        sib_copy(h).wait_send()
 
     for d in (1, 2, 3):
         x_first(d, x).wait_send()
@@ -616,20 +651,21 @@
             pltpu.VMEM((4, part, width // 2), BF),
             pltpu.VMEM((4, part, width // 2), BF),
             pltpu.VMEM((4, part, width // 2), BF),
-            pltpu.VMEM((part, width), F32),
+            pltpu.VMEM((part, width), BF),
+            pltpu.VMEM((part, width), BF),
             pltpu.VMEM((n_e, block, part), BF),
             pltpu.VMEM((n_e, block, part), BF),
             dma((bases // 4,)),
+            dma((n_z, 2)),
+            dma((n_z, 2)),
             dma((n_z,)),
             dma((n_z,)),
-            dma((n_z,)),
-            dma((n_z,)),
-            dma((n_z,)),
-            dma((n_z,)),
+            dma((n_z, 2)),
+            dma((n_z, 2)),
             dma,
             dma,
-            dma,
-            dma,
+            dma((2,)),
+            dma((2,)),
             dma((4,)),
             dma((4,)),
             dma((4,)),

time: 103 us -> 93.5 us (0.908)
  Pallas kernels: 102 us -> 92.7 us
    pallas_call x1, Pallas kernels: 99.5 us -> 90.3 us  [run_step(): pl.pallas_call(functools.partial(step_kernel, n_z, n_e), out_shape=(jax.S...]
where the time goes in v8:
time: 93.5 us; the launch traced here: 93.3 us
  Pallas kernels  92.7 us (99%)
    pallas_call x1, Pallas kernels, run_step(): pl.pallas_call(functools.partial(step_kernel, n_z, n_e), out_shape=(jax.S...  90.3 us
    pallas_call x1, Pallas kernels, store(): pl.pallas_call(store_kernel, out_shape=tuple((jax.ShapeDtypeStruct(a.shap...  2.34 us

profile of v8, /device:TPU:25, one launch (start us, length us, event | category | flops | bytes accessed | tf_op | source)
XLA Modules:
  0.0 93.3 jit_solution(4981596514672930374)
XLA Ops:
  0.6 90.3 %shard_map.121 = (bf16[512,512]{1,0:T(8,128)(2,1)}, bf16[512,512]{1,0:T(8,128)(2,1)}, f32[128,512]{1,0:T(8,128)}) custom-call(s32[1,512]{1,0:T(1,128)} %bitcast.9, s32[1,512]{1,0:T(1,128)} %bitcast.10, s32[1,512]{1,0:T(1,128)} %bitcast.11, s32[1,250]{1,0:T(1,128)} %bitcast.12, s32[1,32]{1,0:T(1,128)} %bitcast.13, bf16[512,512]{1,0:T(8,128)(2,1)} %feat_ref.1, ...), custom_call_target="tpu_custom_call" | custom-call | tf_op jit(solution)/shard_map/pallas_call | solution.py:609
  91.0 2.3 %shard_map.122 = (bf16[512,512]{1,0:T(8,128)(2,1)}, bf16[512,512]{1,0:T(8,128)(2,1)}, f32[128,512]{1,0:T(8,128)}) custom-call(bf16[512,512]{1,0:T(8,128)(2,1)} %get-tuple-element.6.a_in, bf16[512,512]{1,0:T(8,128)(2,1)} %get-tuple-element.7.b_in, f32[128,512]{1,0:T(8,128)} %get-tuple-element.8.c_in), custom_call_target="tpu_custom_call" | custom-call | tf_op jit(solution)/shard_map/pallas_call | solution.py:720

commit v9 on v8

--- a/solution.py
+++ b/solution.py
@@ -490,22 +490,22 @@
         act_copy(d, q).start()
     seg = acc.shape[1]
 
-    def spread(first):
+    def spread(n):
+        at = pl.ds(pl.multiple_of(n * seg, seg), seg)
         acc[...] = jnp.zeros_like(acc)
 
         def step(i, _):
-            out = dot(back[i], pick[:, first : first + seg])
+            out = dot(back[i], pick[:, at])
             rows = acc[...]
             for g in range(group):
-                coef = coef_t_ref[pl.ds(i * group + g, 1), first : first + seg]
-                rows += out[g * part : (g + 1) * part] * coef
+                rows += out[g * part : (g + 1) * part] * coef_t_ref[pl.ds(i * group + g, 1), at]
             acc[...] = rows
             return 0
 
         lax.fori_loop(0, bases // group, step, 0)
         block = row_out.shape[1]
         rows = acc[...].T.astype(BF).reshape(seg // block, block, part)
-        row_out[first // block : (first + seg) // block] = rows
+        row_out[pl.ds(n * (seg // block), seg // block)] = rows
 
     def row_copy(peer, slot):
         return remote(
@@ -520,8 +520,9 @@
         return 0
 
     per_seg = n_e * seg // pick.shape[1]
-    for n in range(n_e // per_seg):
-        spread(n * seg)
+    for d in (2, 1, 3, 0):
+        n = lax.rem(y + d, n_e // per_seg)
+        spread(n)
         lax.fori_loop(n * per_seg, (n + 1) * per_seg, row_start, 0)
     row_in[e] = row_out[e]
 
@@ -552,7 +553,6 @@
 
     for d in range(1, n_z):
         gf_copy(d, q).start()
-
     done[:, :wide] = add_up(half_x[y], xy_in, x_then_y, y).astype(BF)
     done[:, wide:] = add_up(half_y[x], yx_in, y_then_x, x).astype(BF)
     move = remote(done, done_in, move_send, move_recv, to_z, to_e)
@@ -564,35 +564,38 @@
     @pl.when(moves)
     def _():
         move.start()
-        move.wait_send()
-        remote(done, done_in, move_send, move_recv, from_z, from_e).wait_recv()
-
-    gb_ref[...] = done_in[...].astype(F32)
 
     for d in range(1, n_z):
         z = lax.rem(q + d, n_z)
         act_copy(d, z).wait_recv()
-        gf_copy(d, z).wait_recv()
+        act_copy(d, q).wait_send()
+        meta_copy(d, q).wait_send()
         for h in range(2):
             sums_copy(d, q, h).wait_send()
             pre_copy(d, q, h).wait_send()
-        act_copy(d, q).wait_send()
-        gf_copy(d, q).wait_send()
     agg_copy.wait_send()
     for h in range(2):
         sib_copy(h).wait_send()
-
     for d in (1, 2, 3):
         x_first(d, x).wait_send()
         y_first(d, y).wait_send()
         x_then_y(d, y).wait_send()
         y_then_x(d, x).wait_send()
-
-    for d in range(1, n_z):
-        meta_copy(d, q).wait_send()
     sent_all(tag_copy)
     sent_all(feed_copy)
     sent_all(row_copy)
+
+    @pl.when(moves)
+    def _():
+        move.wait_send()
+        remote(done, done_in, move_send, move_recv, from_z, from_e).wait_recv()
+
+    gb_ref[...] = done_in[...].astype(F32)
+
+    for d in range(1, n_z):
+        z = lax.rem(q + d, n_z)
+        gf_copy(d, z).wait_recv()
+        gf_copy(d, q).wait_send()
 
 
 def run_step(src, dst, rel, groups, counts, features, w_self, cotangent, coeffs, basis_mats):
@@ -641,7 +644,7 @@
             pltpu.VMEM((bases, part, width), BF),
             pltpu.VMEM((n_ent, all_slots), BF),
             pltpu.VMEM((n_ent, all_slots), BF),
-            pltpu.VMEM((part, all_slots // 2), F32),
+            pltpu.VMEM((part, all_slots // 4), F32),
             pltpu.VMEM((bases // 4, 4 * part, n_ent), BF),
             pltpu.VMEM((4, 4, part, width // 2), BF),
             pltpu.VMEM((4, 4, part, width // 2), BF),

time: 93.5 us -> 92 us (0.984)
  Pallas kernels: 92.7 us -> 90.8 us
    pallas_call x1, Pallas kernels: 90.3 us -> 88.5 us  [run_step(): pl.pallas_call(functools.partial(step_kernel, n_z, n_e), out_shape=(jax.S...]
where the time goes in v9:
time: 92 us; the launch traced here: 91.5 us
  Pallas kernels  90.8 us (99%)
    pallas_call x1, Pallas kernels, run_step(): pl.pallas_call(functools.partial(step_kernel, n_z, n_e), out_shape=(jax.S...  88.5 us
    pallas_call x1, Pallas kernels, store(): pl.pallas_call(store_kernel, out_shape=tuple((jax.ShapeDtypeStruct(a.shap...  2.34 us

profile of v9, /device:TPU:25, one launch (start us, length us, event | category | flops | bytes accessed | tf_op | source)
XLA Modules:
  0.0 91.5 jit_solution(3039098319452746599)
XLA Ops:
  0.6 88.5 %shard_map.121 = (bf16[512,512]{1,0:T(8,128)(2,1)}, bf16[512,512]{1,0:T(8,128)(2,1)}, f32[128,512]{1,0:T(8,128)}) custom-call(s32[1,512]{1,0:T(1,128)} %bitcast.9, s32[1,512]{1,0:T(1,128)} %bitcast.10, s32[1,512]{1,0:T(1,128)} %bitcast.11, s32[1,250]{1,0:T(1,128)} %bitcast.12, s32[1,32]{1,0:T(1,128)} %bitcast.13, bf16[512,512]{1,0:T(8,128)(2,1)} %feat_ref.1, ...), custom_call_target="tpu_custom_call" | custom-call | tf_op jit(solution)/shard_map/pallas_call | solution.py:612
  89.1 2.3 %shard_map.122 = (bf16[512,512]{1,0:T(8,128)(2,1)}, bf16[512,512]{1,0:T(8,128)(2,1)}, f32[128,512]{1,0:T(8,128)}) custom-call(bf16[512,512]{1,0:T(8,128)(2,1)} %get-tuple-element.6.a_in, bf16[512,512]{1,0:T(8,128)(2,1)} %get-tuple-element.7.b_in, f32[128,512]{1,0:T(8,128)} %get-tuple-element.8.c_in), custom_call_target="tpu_custom_call" | custom-call | tf_op jit(solution)/shard_map/pallas_call | solution.py:723

commit v10 on v9

--- a/solution.py
+++ b/solution.py
@@ -707,15 +707,21 @@
     )
 
 
-def store_kernel(a_in, b_in, c_in, a_out, b_out, c_out, sems):
-    copies = [
-        pltpu.make_async_copy(i, o, sems.at[n])
-        for n, (i, o) in enumerate(((a_in, a_out), (b_in, b_out), (c_in, c_out)))
+def store_kernel(a_in, b_in, c_in, a_out, b_out, c_out, a_mid, b_mid, c_mid, sems):
+    arrays = ((c_in, c_mid, c_out), (a_in, a_mid, a_out), (b_in, b_mid, b_out))
+    loads = [
+        pltpu.make_async_copy(i, m, sems.at[0, n]) for n, (i, m, _) in enumerate(arrays)
     ]
-    for copy in copies:
-        copy.start()
-    for copy in copies:
-        copy.wait()
+    stores = [
+        pltpu.make_async_copy(m, o, sems.at[1, n]) for n, (_, m, o) in enumerate(arrays)
+    ]
+    for load in loads:
+        load.start()
+    for load, save in zip(loads, stores):
+        load.wait()
+        save.start()
+    for save in stores:
+        save.wait()
 
 
 def store(arrays):
@@ -723,9 +729,10 @@
     return pl.pallas_call(
         store_kernel,
         out_shape=tuple(jax.ShapeDtypeStruct(a.shape, a.dtype) for a in arrays),
-        in_specs=[pl.BlockSpec(memory_space=pltpu.VMEM)] * 3,
+        in_specs=[hbm] * 3,
         out_specs=(hbm,) * 3,
-        scratch_shapes=[pltpu.SemaphoreType.DMA((3,))],
+        scratch_shapes=[pltpu.VMEM(a.shape, a.dtype) for a in arrays]
+        + [pltpu.SemaphoreType.DMA((2, 3))],
     )(*arrays)
 
 

time: 92 us -> 91.8 us (level)
  no operation moved by 1% of the time
where the time goes in v10:
time: 91.8 us; the launch traced here: 91.3 us
  Pallas kernels  90.6 us (99%)
    pallas_call x1, Pallas kernels, run_step(): pl.pallas_call(functools.partial(step_kernel, n_z, n_e), out_shape=(jax.S...  88.5 us
    pallas_call x1, Pallas kernels, store(): pl.pallas_call(store_kernel, out_shape=tuple((jax.ShapeDtypeStruct(a.shap...  2.14 us

profile of v10, /device:TPU:25, one launch (start us, length us, event | category | flops | bytes accessed | tf_op | source)
XLA Modules:
  0.0 91.3 jit_solution(9252560247987874054)
XLA Ops:
  0.6 88.5 %shard_map.121 = (bf16[512,512]{1,0:T(8,128)(2,1)}, bf16[512,512]{1,0:T(8,128)(2,1)}, f32[128,512]{1,0:T(8,128)}) custom-call(s32[1,512]{1,0:T(1,128)} %bitcast.9, s32[1,512]{1,0:T(1,128)} %bitcast.10, s32[1,512]{1,0:T(1,128)} %bitcast.11, s32[1,250]{1,0:T(1,128)} %bitcast.12, s32[1,32]{1,0:T(1,128)} %bitcast.13, bf16[512,512]{1,0:T(8,128)(2,1)} %feat_ref.1, ...), custom_call_target="tpu_custom_call" | custom-call | tf_op jit(solution)/shard_map/pallas_call | solution.py:612
  89.1 2.1 %shard_map.122 = (bf16[512,512]{1,0:T(8,128)(2,1)}, bf16[512,512]{1,0:T(8,128)(2,1)}, f32[128,512]{1,0:T(8,128)}) custom-call(bf16[512,512]{1,0:T(8,128)(2,1)} %get-tuple-element.6.a_in, bf16[512,512]{1,0:T(8,128)(2,1)} %get-tuple-element.7.b_in, f32[128,512]{1,0:T(8,128)} %get-tuple-element.8.c_in), custom_call_target="tpu_custom_call" | custom-call | tf_op jit(solution)/shard_map/pallas_call | solution.py:729
